TPU v7x, 32 devices: a whole 2x2x4 slice. The times are simulated.
32 devices in a mesh: lat: 4 (over y, x), lon: 8 (over z, core).
Axes of the slice: x: 2, y: 2, z: 4, core: 2. Of those that a mesh axis runs over, the one named last changes fastest.
Arguments:
- grid_state: float32 [48, 120, 384], P('lat', 'lon'), may hold values from -6 to 6
- norm_gain: float32 [2, 384], replicated, may hold values from 0.25 to 1.75
- conv_weight: bfloat16 [2, 3, 3, 384, 384], replicated, may hold values from -0.109375 to 0.109375
- filter_weight: bfloat16 [48, 384, 384], P('lat'), may hold values from -0.3125 to 0.3125
- degree_keep: int32 [48, 48], P('lat', 'lon'), may hold values 0 or 1
Outputs:
- updated: float32 [48, 120, 384], P('lat', 'lon')
Inputs may be any that keep to these rules, and one draw needn't show every extreme that they name: degree_keep[l, m] is 0 or 1 for degree l and order m.
All inputs are finite; a program needn't handle non-finite values. No bound on the sum of `degree_keep` on one device may be relied on, other than what follows from the above.
Results may differ from a plain program's by a relative error of at most 0.008.
Values may be sent and summed in bfloat16 or wider, within the bound.
A program may use at most 64 MiB of HBM per device.

v0:
```python
import math

import jax
import jax.numpy as jnp
from jax import lax
from jax.sharding import PartitionSpec as P

epsilon = 1e-06


def extended(array, sides, width):
    for axis, dim in sides:
        size, length = (lax.axis_size(axis), array.shape[dim])
        up = [(i, (i + 1) % size) for i in range(size)]
        down = [(j, i) for i, j in up]
        last = lax.slice_in_dim(array, length - width, length, axis=dim)
        first = lax.slice_in_dim(array, 0, width, axis=dim)
        before = lax.ppermute(last, axis, up)
        after = lax.ppermute(first, axis, down)
        array = jnp.concatenate([before, array, after], axis=dim)
    return array


def colatitude(row_index, total_rows, float_type):
    theta_rows = (row_index.astype(float_type) + 0.5) * (math.pi / total_rows)
    return (jnp.cos(theta_rows), jnp.sin(theta_rows))


def legendre_table(orders, cosine, sine_values, amount):
    float_type = cosine.dtype
    order_f = orders.astype(float_type)[:, None]
    order_i = orders[:, None]
    column = cosine[None, :]
    log_start = (
        0.5
        * (
            jnp.log((2.0 * order_f + 1.0) / (4.0 * math.pi))
            + jax.scipy.special.gammaln(order_f + 0.5)
            - jax.scipy.special.gammaln(order_f + 1.0)
            - 0.5 * math.log(math.pi)
        )
        + order_f * jnp.log(sine_values)[None, :]
    )
    sectoral = jnp.exp(log_start)

    def advance(carry, degree):
        before, latest = carry
        degree_f = degree.astype(float_type)
        growth = jnp.sqrt(
            jnp.maximum(4.0 * degree_f * degree_f - 1.0, 1.0)
            / jnp.maximum(degree_f * degree_f - order_f * order_f, 1.0)
        )
        prior = degree_f - 1.0
        damping = jnp.sqrt(
            jnp.maximum(prior * prior - order_f * order_f, 0.0)
            / jnp.maximum(4.0 * prior * prior - 1.0, 1.0)
        )
        grown = growth * (column * latest - damping * before)
        fresh = jnp.where(
            degree < order_i, jnp.zeros_like(grown), jnp.where(degree == order_i, sectoral, grown)
        )
        return ((latest, fresh), fresh)

    zero_rows = jnp.zeros((orders.shape[0], cosine.shape[0]), float_type)
    _, assoc_basis = lax.scan(
        advance, (zero_rows, zero_rows), jnp.arange(amount, dtype=jnp.int32), unroll=16
    )
    return assoc_basis


def forward_table(columns, modes, total_cols, float_type):
    lon_index = columns[:, None]
    order_index = jnp.arange(modes, dtype=jnp.int32)[None, :]
    phase = (lon_index * order_index % total_cols).astype(float_type) * (2.0 * math.pi / total_cols)
    factor = 2.0 * math.pi / total_cols
    return jnp.stack([jnp.cos(phase) * factor, -jnp.sin(phase) * factor], axis=2).reshape(
        columns.shape[0], 2 * modes
    )


def inverse_table(modes, total_cols, float_type):
    order_index = jnp.arange(modes, dtype=jnp.int32)[:, None]
    lon_index = jnp.arange(total_cols, dtype=jnp.int32)[None, :]
    phase = (lon_index * order_index % total_cols).astype(float_type) * (2.0 * math.pi / total_cols)
    factor = jnp.where(order_index == 0, 1.0, 2.0).astype(float_type)
    return jnp.stack([jnp.cos(phase) * factor, -jnp.sin(phase) * factor], axis=1).reshape(
        2 * modes, total_cols
    )


def paired(form, data, table):
    upper_part = table.astype(jnp.bfloat16)
    lower_part = (table - upper_part.astype(jnp.float32)).astype(jnp.bfloat16)
    first = jnp.einsum(form, data, upper_part, preferred_element_type=jnp.float32)
    return first + jnp.einsum(form, data, lower_part, preferred_element_type=jnp.float32)


def to_columns(values):
    return lax.all_to_all(values, "lon", split_axis=2, concat_axis=0, tiled=True)


def to_channels(values):
    return lax.all_to_all(values, "lon", split_axis=0, concat_axis=2, tiled=True)


def grid_rims(normed):
    padded = extended(normed, (("lat", 0), ("lon", 1)), 1)
    place = lax.axis_index("lat")
    final_place = lax.axis_size("lat") - 1
    zero_line = jnp.zeros_like(padded[:1])
    upper_rim = jnp.where(place == 0, zero_line, padded[:1])
    lower_rim = jnp.where(place == final_place, zero_line, padded[-1:])
    return jnp.concatenate([upper_rim, padded[1:-1], lower_rim], axis=0)


def conv_taps(padded, weight, row_count, col_count):
    channels = padded.shape[2]
    running = jnp.zeros((row_count * col_count, weight.shape[3]), jnp.float32)
    for row_tap in range(3):
        for col_tap in range(3):
            window = padded[row_tap : row_tap + row_count, col_tap : col_tap + col_count].reshape(
                row_count * col_count, channels
            )
            running = running + jnp.dot(
                window, weight[row_tap, col_tap], preferred_element_type=jnp.float32
            )
    return running.reshape(row_count, col_count, weight.shape[3])


def conv_block(grid_state, gain, weight):
    row_count, col_count, channels = grid_state.shape
    scale_rows = lax.rsqrt(jnp.mean(grid_state * grid_state, axis=-1, keepdims=True) + epsilon)
    normed = (grid_state * scale_rows * gain).astype(jnp.bfloat16)
    padded = grid_rims(normed)
    mixture = conv_taps(padded, weight, row_count, col_count)
    return grid_state + jax.nn.gelu(mixture, approximate=False)


def per_device(grid_state, norm_gain, conv_weight, filter_weight, degree_keep):
    f32 = jnp.float32
    for depth_index in range(2):
        grid_state = conv_block(grid_state, norm_gain[depth_index], conv_weight[depth_index])
    row_count, col_count, channels = grid_state.shape
    lat_parts = lax.axis_size("lat")
    lon_parts = lax.axis_size("lon")
    total_rows = row_count * lat_parts
    total_cols = col_count * lon_parts
    local_modes = total_rows // lon_parts
    share = channels // lon_parts
    columns = to_columns(jnp.transpose(grid_state.astype(jnp.bfloat16), (1, 0, 2)))
    flat_columns = columns.reshape(total_cols, row_count * share)
    dft_table = forward_table(jnp.arange(total_cols), total_rows, total_cols, f32)
    spectrum = paired("lx,lk->kx", flat_columns, dft_table).astype(jnp.bfloat16)
    spectrum = to_channels(spectrum.reshape(2 * total_rows, row_count, share))
    spectrum = jnp.transpose(spectrum, (1, 0, 2)).reshape(row_count, local_modes, 2 * channels)
    orders = lax.axis_index("lon") * local_modes + jnp.arange(local_modes, dtype=jnp.int32)
    keep_mask = degree_keep.astype(f32)
    cosine, sine_values = colatitude(jnp.arange(total_rows), total_rows, f32)
    assoc_basis = legendre_table(orders, cosine, sine_values, total_rows)
    weighted = assoc_basis * (sine_values * (math.pi / total_rows))[None, None, :]
    first_here = lax.axis_index("lat") * row_count
    own_weighted = lax.dynamic_slice_in_dim(weighted, first_here, row_count, 0)
    own_rows_basis = lax.dynamic_slice_in_dim(assoc_basis, first_here, row_count, 2)
    basis_rows = own_weighted
    coefficients = paired(
        "imx,lmi->lmx", lax.all_gather(spectrum, "lat", axis=0, tiled=True), basis_rows
    ).astype(jnp.bfloat16)
    flat_coeffs = coefficients.reshape(row_count, 2 * local_modes, channels)
    mixture = jnp.einsum("lkc,lcd->lkd", flat_coeffs, filter_weight, preferred_element_type=f32)
    mixture = mixture.reshape(row_count, local_modes, 2, channels) * keep_mask[:, :, None, None]
    filtered = mixture.reshape(row_count, local_modes, 2 * channels).astype(jnp.bfloat16)
    basis_rows = own_rows_basis
    synthesis = paired(
        "lmx,lmi->imx", lax.all_gather(filtered, "lat", axis=0, tiled=True), basis_rows
    ).astype(jnp.bfloat16)
    by_order = jnp.transpose(synthesis.reshape(row_count, 2 * local_modes, channels), (1, 0, 2))
    returned = to_columns(by_order)
    flat_returned = returned.reshape(2 * total_rows, row_count * share)
    physical = paired(
        "kx,kl->lx", flat_returned, inverse_table(total_rows, total_cols, f32)
    ).astype(jnp.bfloat16)
    physical = to_channels(physical.reshape(total_cols, row_count, share))
    physical = jnp.transpose(physical, (1, 0, 2))
    return grid_state + jax.nn.gelu(physical.astype(f32), approximate=False)


def solution(mesh):
    in_specs = (P("lat", "lon", None), P(), P(), P("lat", None, None), P("lat", "lon"))
    out_specs = P("lat", "lon", None)
    return jax.shard_map(
        per_device, mesh=mesh, in_specs=in_specs, out_specs=out_specs, check_vma=False
    )
```

profile of v0, /device:TPU:0, one launch (start us, length us, event | category | flops | bytes accessed | tf_op | source)
XLA Modules:
  0.0 426.2 jit_solution(8437420346642597354)
XLA Ops:
  4.9 3.0 collective-permute-start
  11.8 5.6 %slice_bitcast_fusion = (bf16[3,3,384,384]{3,2,1,0:T(8,128)(2,1)}, bf16[3,3,384,384]{3,2,1,0:T(8,128)(2,1)}) fusion(bf16[2,3,3,384,384]{4,3,2,1,0:T(8,128)(2,1)} %param.9), kind=kLoop, calls=%fused_computation.125 | loop fusion | bytes 10616832 | tf_op jit(solution)/shard_map/squeeze | solution.py:142
  17.4 152.1 %while.21 = (s32[]{:T(128)}, f32[6,48]{1,0:T(8,128)}, f32[6,48]{1,0:T(8,128)}, f32[3,16,6,48]{3,2,1,0:T(8,128)}, s32[3,16]{1,0:T(4,128)}, /*index=5*/s32[]{:T(12...) while((s32[]{:T(128)}, f32[6,48]{1,0:T(8,128)}, ...), condition=%wide.region_3.4_spmd.clone.clone.clone.clone, body=%wide.region_2.3_spmd.clone.clone.clone.clone.sunk | while | flops 65138 | bytes 363896 | solution.py:65
  174.8 3.5 collective-permute-start.3
  224.2 3.5 collective-permute-start.7
  264.1 2.5 convert_bitcast_fusion
  266.6 2.8 copy.96
  269.4 3.5 reshape.1588
  272.9 4.0 all-to-all-start
  283.8 3.5 reshape.1589
  287.3 3.4 copy.97
  301.3 4.3 %all-to-all-start.1 = ((bf16[8,2,3456]{2,1,0:T(2,128)(2,1)}), bf16[8,2,3456]{2,1,0:T(2,128)(2,1)}, u32[]{:S(2)}, u32[]{:S(2)}) async-start(bf16[8,2,3456]{2,1,0:T(2,128)(2,1)} %reshape.1590), calls=%async_computation.1 | async-start | bytes 221184 | tf_op jit(solution)/shard_map/all_to_all | solution.py:103
  306.4 5.8 %all-to-all-done.1 = bf16[8,2,3456]{2,1,0:T(2,128)(2,1)} async-done(((bf16[8,2,3456]{2,1,0:T(2,128)(2,1)}), bf16[8,2,3456]{2,1,0:T(2,128)(2,1)}, u32[]{:S(2)}, u32[]{:S(2)}) %all-to-all-start.1) | async-done | bytes 110624 | tf_op jit(solution)/shard_map/all_to_all | solution.py:103
  321.4 11.5 %all_gather.6 = bf16[48,6,768]{2,1,0:T(8,128)(2,1)S(1)} all-gather(bf16[12,6,768]{2,1,0:T(8,128)(2,1)} %reshape.1571), channel_id=1, replica_groups=mesh['lat'=4,'lon'=8] {'lat'}, dimensions={0}, use_global_device_ids=true | all-gather | bytes 552960 | tf_op jit(solution)/shard_map/all_gather | solution.py:166
  337.4 2.2 fusion.151
  342.4 10.4 %all_gather.7 = bf16[48,6,768]{2,1,0:T(8,128)(2,1)S(1)} all-gather(bf16[12,6,768]{2,1,0:T(8,128)(2,1)S(1)} %multiply_convert_fusion), channel_id=1, replica_groups=mesh['lat'=4,'lon'=8] {'lat'}, dimensions={0}, use_global_device_ids=true | all-gather | bytes 552960 | tf_op jit(solution)/shard_map/all_gather | solution.py:174
  357.2 2.8 copy.111
  360.0 3.4 reshape.1592
  363.4 4.0 all-to-all-start.2
  370.2 3.7 all-to-all-done.2
  373.9 3.4 reshape.1593
  377.3 3.2 copy.112
  389.8 10.8 %all_to_all.57 = bf16[8,2,4320]{2,1,0:T(2,128)(2,1)} all-to-all(bf16[8,2,4320]{2,1,0:T(2,128)(2,1)} %reshape.1594), channel_id=1, replica_groups=mesh['lat'=4,'lon'=8] {'lon'}, dimensions={0} | all-to-all | bytes 276480 | tf_op jit(solution)/shard_map/all_to_all | solution.py:103
  423.7 2.5 fusion.67
  (468 shorter events, 291.1 us)
Async XLA Ops:
  0.0 337.4 %copy-start = (bf16[12,384,384]{2,1,0:T(8,128)(2,1)S(1)}, bf16[12,384,384]{2,1,0:T(8,128)(2,1)}, u32[]{:S(2)}) copy-start(bf16[12,384,384]{2,1,0:T(8,128)(2,1)} %param.10) | copy-start | bytes 10616836
  4.9 168.3 %collective-permute-start = (bf16[1,15,384]{2,1,0:T(8,128)(2,1)}, bf16[1,15,384]{2,1,0:T(8,128)(2,1)}, u32[]{:S(2)}, u32[]{:S(2)}) collective-permute-start(bf16[1,15,384]{2,1,0:T(8,128)(2,1)} %get-tuple-element.566), channel_id=1, source_target_pairs={{0,8},{8,16},{16,24},{24,0},{1,9},{9,17},{17,25},{25,1},{2,10},{10... | collective-permute-start | bytes 34568 | tf_op jit(solution)/shard_map/ppermute | solution.py:18
  7.8 165.4 %collective-permute-start.1 = (bf16[1,15,384]{2,1,0:T(8,128)(2,1)}, bf16[1,15,384]{2,1,0:T(8,128)(2,1)}, u32[]{:S(2)}, u32[]{:S(2)}) collective-permute-start(bf16[1,15,384]{2,1,0:T(8,128)(2,1)} %get-tuple-element.567), channel_id=1, source_target_pairs={{8,0},{16,8},{24,16},{0,24},{9,1},{17,9},{25,17},{1,25},{10,2},{18... | collective-permute-start | bytes 34568 | tf_op jit(solution)/shard_map/ppermute | solution.py:19
  42.2 6.6 %copy-start.25 = (f32[6]{0:T(128)}, f32[6]{0:T(128)S(1)}, u32[]{:S(2)}) copy-start(f32[6]{0:T(128)S(1)} %get-tuple-element.771) | copy-start | bytes 76 | tf_op jit(solution)/shard_map/while
  50.2 4.5 %copy-start.6 = (f32[6,48]{1,0:T(8,128)}, f32[6,48]{1,0:T(8,128)S(1)}, u32[]{:S(2)}) copy-start(f32[6,48]{1,0:T(8,128)S(1)} %get-tuple-element.790) | copy-start | bytes 3460 | tf_op jit(solution)/shard_map/while
  92.9 6.6 %copy-start.25 = (f32[6]{0:T(128)}, f32[6]{0:T(128)S(1)}, u32[]{:S(2)}) copy-start(f32[6]{0:T(128)S(1)} %get-tuple-element.771) | copy-start | bytes 76 | tf_op jit(solution)/shard_map/while
  100.9 4.5 %copy-start.6 = (f32[6,48]{1,0:T(8,128)}, f32[6,48]{1,0:T(8,128)S(1)}, u32[]{:S(2)}) copy-start(f32[6,48]{1,0:T(8,128)S(1)} %get-tuple-element.790) | copy-start | bytes 3460 | tf_op jit(solution)/shard_map/while
  143.6 6.6 %copy-start.25 = (f32[6]{0:T(128)}, f32[6]{0:T(128)S(1)}, u32[]{:S(2)}) copy-start(f32[6]{0:T(128)S(1)} %get-tuple-element.771) | copy-start | bytes 76 | tf_op jit(solution)/shard_map/while
  151.6 4.5 %copy-start.6 = (f32[6,48]{1,0:T(8,128)}, f32[6,48]{1,0:T(8,128)S(1)}, u32[]{:S(2)}) copy-start(f32[6,48]{1,0:T(8,128)S(1)} %get-tuple-element.790) | copy-start | bytes 3460 | tf_op jit(solution)/shard_map/while
  174.8 5.3 %collective-permute-start.2 = (bf16[14,1,384]{2,1,0:T(2,128)(2,1)}, bf16[14,1,384]{2,1,0:T(2,128)(2,1)}, u32[]{:S(2)}, u32[]{:S(2)}) collective-permute-start(bf16[14,1,384]{2,1,0:T(2,128)(2,1)} %get-tuple-element.560), channel_id=1, source_target_pairs={{0,1},{1,2},{2,3},{3,4},{4,5},{5,6},{6,7},{7,0},{8,9},{9,10},{10,1... | collective-permute-start | bytes 32264 | tf_op jit(solution)/shard_map/ppermute | solution.py:18
  174.8 5.3 %collective-permute-start.3 = (bf16[14,1,384]{2,1,0:T(2,128)(2,1)}, bf16[14,1,384]{2,1,0:T(2,128)(2,1)}, u32[]{:S(2)}, u32[]{:S(2)}) collective-permute-start(bf16[14,1,384]{2,1,0:T(2,128)(2,1)} %get-tuple-element.561), channel_id=1, source_target_pairs={{1,0},{2,1},{3,2},{4,3},{5,4},{6,5},{7,6},{0,7},{9,8},{10,9},{11,1... | collective-permute-start | bytes 32264 | tf_op jit(solution)/shard_map/ppermute | solution.py:19
  201.9 5.4 %copy-start.13 = (bf16[180,384]{1,0:T(8,128)(2,1)S(1)}, bf16[180,384]{1,0:T(8,128)(2,1)}, u32[]{:S(2)}) copy-start(bf16[180,384]{1,0:T(8,128)(2,1)} %reshape.1554) | copy-start | bytes 414724
  201.9 6.6 %copy-start.9 = (bf16[180,384]{1,0:T(8,128)(2,1)S(1)}, bf16[180,384]{1,0:T(8,128)(2,1)}, u32[]{:S(2)}) copy-start(bf16[180,384]{1,0:T(8,128)(2,1)} %reshape.1555) | copy-start | bytes 414724
  206.1 9.8 %copy-start.38 = (f32[384]{0:T(512)S(1)}, f32[384]{0:T(512)}, u32[]{:S(2)}) copy-start(f32[384]{0:T(512)} %get-tuple-element.402) | copy-start | bytes 4612
  217.2 5.9 %collective-permute-start.4 = (bf16[1,15,384]{2,1,0:T(8,128)(2,1)}, bf16[1,15,384]{2,1,0:T(8,128)(2,1)S(1)}, u32[]{:S(2)}, u32[]{:S(2)}) collective-permute-start(bf16[1,15,384]{2,1,0:T(8,128)(2,1)} %get-tuple-element.564), channel_id=1, source_target_pairs={{0,8},{8,16},{16,24},{24,0},{1,9},{9,17},{17,25},{25,1},{2,10},{10... | collective-permute-start | bytes 34568 | tf_op jit(solution)/shard_map/ppermute | solution.py:18
  218.3 4.8 %collective-permute-start.5 = (bf16[1,15,384]{2,1,0:T(8,128)(2,1)}, bf16[1,15,384]{2,1,0:T(8,128)(2,1)}, u32[]{:S(2)}, u32[]{:S(2)}) collective-permute-start(bf16[1,15,384]{2,1,0:T(8,128)(2,1)} %get-tuple-element.565), channel_id=1, source_target_pairs={{8,0},{16,8},{24,16},{0,24},{9,1},{17,9},{25,17},{1,25},{10,2},{18... | collective-permute-start | bytes 34568 | tf_op jit(solution)/shard_map/ppermute | solution.py:19
  224.1 5.6 %collective-permute-start.6 = (bf16[14,1,384]{2,1,0:T(2,128)(2,1)S(1)}, bf16[14,1,384]{2,1,0:T(2,128)(2,1)S(1)}, u32[]{:S(2)}, u32[]{:S(2)}) collective-permute-start(bf16[14,1,384]{2,1,0:T(2,128)(2,1)S(1)} %get-tuple-element.556), channel_id=1, source_target_pairs={{0,1},{1,2},{2,3},{3,4},{4,5},{5,6},{6,7},{7,0},{8,9},{9,10},{10,1... | collective-permute-start | bytes 32264 | tf_op jit(solution)/shard_map/ppermute | solution.py:18
  224.2 5.5 %collective-permute-start.7 = (bf16[14,1,384]{2,1,0:T(2,128)(2,1)S(1)}, bf16[14,1,384]{2,1,0:T(2,128)(2,1)S(1)}, u32[]{:S(2)}, u32[]{:S(2)}) collective-permute-start(bf16[14,1,384]{2,1,0:T(2,128)(2,1)S(1)} %get-tuple-element.557), channel_id=1, source_target_pairs={{1,0},{2,1},{3,2},{4,3},{5,4},{6,5},{7,6},{0,7},{9,8},{10,9},{11,1... | collective-permute-start | bytes 32264 | tf_op jit(solution)/shard_map/ppermute | solution.py:19
  252.0 5.4 %copy-start.14 = (bf16[180,384]{1,0:T(8,128)(2,1)S(1)}, bf16[180,384]{1,0:T(8,128)(2,1)}, u32[]{:S(2)}) copy-start(bf16[180,384]{1,0:T(8,128)(2,1)} %reshape.1563) | copy-start | bytes 414724
  252.0 6.6 %copy-start.10 = (bf16[180,384]{1,0:T(8,128)(2,1)S(1)}, bf16[180,384]{1,0:T(8,128)(2,1)}, u32[]{:S(2)}) copy-start(bf16[180,384]{1,0:T(8,128)(2,1)} %reshape.1564) | copy-start | bytes 414724
  264.1 17.1 %copy-start.39 = (s32[12,6]{0,1:T(8,128)S(1)}, s32[12,6]{0,1:T(8,128)}, u32[]{:S(2)}) copy-start(s32[12,6]{0,1:T(8,128)} %param.11) | copy-start | bytes 868
  272.9 10.9 %all-to-all-start = ((bf16[8,2,4320]{2,1,0:T(2,128)(2,1)}), bf16[8,2,4320]{2,1,0:T(2,128)(2,1)}, u32[]{:S(2)}, u32[]{:S(2)}) async-start(bf16[8,2,4320]{2,1,0:T(2,128)(2,1)} %reshape.1588), calls=%async_computation | async-start | bytes 278528 | tf_op jit(solution)/shard_map/all_to_all | solution.py:99
  301.3 10.9 %all-to-all-start.1 = ((bf16[8,2,3456]{2,1,0:T(2,128)(2,1)}), bf16[8,2,3456]{2,1,0:T(2,128)(2,1)}, u32[]{:S(2)}, u32[]{:S(2)}) async-start(bf16[8,2,3456]{2,1,0:T(2,128)(2,1)} %reshape.1590), calls=%async_computation.1 | async-start | bytes 221184 | tf_op jit(solution)/shard_map/all_to_all | solution.py:103
  363.4 10.5 %all-to-all-start.2 = ((bf16[8,2,3456]{2,1,0:T(2,128)(2,1)}), bf16[8,2,3456]{2,1,0:T(2,128)(2,1)}, u32[]{:S(2)}, u32[]{:S(2)}) async-start(bf16[8,2,3456]{2,1,0:T(2,128)(2,1)} %reshape.1592), calls=%async_computation.2 | async-start | bytes 221184 | tf_op jit(solution)/shard_map/all_to_all | solution.py:99
  (75 other events, 199.0 us)
where the time goes:
time: 432 us; the launch traced here: 426 us
  other arithmetic  142 us (33%)
  local copies, waits for them, and re-layouts  140 us (32%)
  matrix products  41.5 us (10%)
  blocking collectives  32.7 us (8%)
  loops' own time  31.1 us (7%)
  starting transfers between devices  26.3 us (6%)
  waiting for transfers between devices  11.3 us (3%)
    while x45, other arithmetic  62.3 us
    eq x48, other arithmetic, advance(): degree == order_i  31.6 us
    another operation x1, loops' own time, legendre_table(): lax.scan(advance, (zero_rows, zero_rows), jnp.arange(amount, dtype=jnp.in...  31.1 us
    dot_general x18, matrix products, conv_taps(): jnp.dot(window, weight[row_tap, col_tap], preferred_element_type=jnp.floa...  29.2 us
    reshape x18, local copies, waits for them, and re-layouts, conv_taps(): padded[row_tap:row_tap + row_count, col_tap:col_tap + col_count]  29.2 us
    unnamed x41, local copies, waits for them, and re-layouts  26.1 us
    mul x8, local copies, waits for them, and re-layouts, per_device(): return grid_state + jax.nn.gelu(physical.astype(f32), approximate=False)  17.1 us
    sqrt x27, other arithmetic, advance(): jnp.sqrt(jnp.maximum(prior * prior - order_f * order_f, 0.0) / jnp.maximu...  13.6 us
  transfers between devices with their start and end apart: 11, of which 4 were waited for; matrix products, arithmetic and copies ran while one was open for 35% of the time, Pallas kernels for 0%

commit v1 on v0

v1 whole, which is shorter than its diff:
```python
import functools
import math

import jax
import jax.numpy as jnp
import ml_dtypes
import numpy as np
from jax import lax
from jax.experimental import pallas as pl
from jax.experimental.pallas import tpu as pltpu
from jax.sharding import PartitionSpec as P

epsilon = 1e-06
LANES = 128
MESH = pl.DeviceIdType.MESH
f32 = jnp.float32
bf16 = jnp.bfloat16


def up(value, step):
    return -(-value // step) * step


def gelu(value):
    return 0.5 * value * (1.0 + lax.erf(value * math.sqrt(0.5)))


def split(table):
    upper = table.astype(ml_dtypes.bfloat16)
    lower = (table - upper.astype(np.float64)).astype(ml_dtypes.bfloat16)
    return np.stack([upper, lower])


def fourier_tables(lon_parts, cols, col_pad, orders, mode_pad):
    total = lon_parts * cols
    forward = np.zeros((lon_parts, mode_pad, lon_parts, col_pad))
    inverse = np.zeros((lon_parts, col_pad, lon_parts, mode_pad))
    m = np.arange(lon_parts * orders)[:, None]
    j = np.arange(total)[None, :]
    phase = (m * j % total) * (2.0 * math.pi / total)
    pair = np.stack([np.cos(phase), -np.sin(phase)], axis=1)
    pair = pair.reshape(lon_parts, 2 * orders, lon_parts, cols)
    weight = np.where(m == 0, 1.0, 2.0)[:, :, None]
    back = (np.stack([np.cos(phase), -np.sin(phase)], axis=1) * weight).reshape(pair.shape)
    forward[:, : 2 * orders, :, :cols] = pair * (2.0 * math.pi / total)
    inverse[:, :cols, :, : 2 * orders] = back.transpose(2, 3, 0, 1)
    side_m, side_c = lon_parts * mode_pad, lon_parts * col_pad
    return split(forward.reshape(side_m, side_c)), split(inverse.reshape(side_c, side_m))


def legendre_seeds(lon_parts, orders, mode_pad, degrees, rows):
    count = lon_parts * orders
    m = np.arange(count, dtype=np.float64)[:, None]
    l = np.arange(degrees, dtype=np.float64)[None, :]
    theta = (np.arange(rows) + 0.5) * (math.pi / rows)
    gammas = np.array([math.lgamma(v + 0.5) - math.lgamma(v + 1.0) for v in range(count)])
    log_start = 0.5 * (
        np.log((2.0 * m + 1.0) / (4.0 * math.pi)) + gammas[:, None] - 0.5 * math.log(math.pi)
    ) + m * np.log(np.sin(theta))[None, :]
    growth = np.where(
        l > m, np.sqrt(np.maximum(4 * l * l - 1, 1) / np.maximum(l * l - m * m, 1)), 0.0
    )
    prior = l - 1.0
    damping = np.sqrt(
        np.maximum(prior * prior - m * m, 0) / np.maximum(4 * prior * prior - 1, 1)
    )
    table = np.concatenate([growth, damping, (l == m) * 1.0, np.exp(log_start)], axis=1)
    table = np.repeat(table.reshape(lon_parts, orders, -1), 2, axis=1)
    full = np.zeros((lon_parts, mode_pad, table.shape[2]), np.float32)
    full[:, : 2 * orders] = table
    lines = np.stack([np.cos(theta), np.sin(theta) * (math.pi / rows)]).astype(np.float32)
    return full, np.concatenate([lines, np.zeros((6, rows), np.float32)])


def conv_kernel(
    lat_parts, lon_parts, chunk,
    x_ref, gain_ref, w_hbm, out_ref, flat_ref,
    state, taps, weights, col_send, col_recv, row_recv, corners,
    w_sem, send_sem, recv_sem,
):
    rows, cols, channels = x_ref.shape
    pad = state.shape[1]
    col_rows = col_send.shape[2]
    lat, lon = lax.axis_index("lat"), lax.axis_index("lon")
    loads = [
        pltpu.make_async_copy(w_hbm.at[k], weights.at[k], w_sem.at[k]) for k in range(2)
    ]
    for load in loads:
        load.start()
    north = lax.rem(lat + lat_parts - 1, lat_parts)
    south = lax.rem(lat + 1, lat_parts)
    west = lax.rem(lon + lon_parts - 1, lon_parts)
    east = lax.rem(lon + 1, lon_parts)
    around = [
        (north, lon), (south, lon), (lat, west), (lat, east),
        (north, west), (south, west), (north, east), (south, east),
    ]
    barrier = pltpu.get_barrier_semaphore()
    for device in around:
        pl.semaphore_signal(barrier, inc=1, device_id=device, device_id_type=MESH)
    spot = lax.broadcasted_iota(jnp.int32, (pad, channels), 0)
    for r in range(rows):
        state[r, pl.ds(cols, pad - cols), :] = jnp.zeros((pad - cols, channels), f32)
        state[r, pl.ds(0, cols), :] = x_ref[r]
    col_send[...] = jnp.zeros(col_send.shape, f32)

    for k in range(2):
        gain = gain_ref[k : k + 1, :]
        for r in range(rows):
            value = state[r]
            scale = lax.rsqrt(jnp.mean(value * value, axis=-1, keepdims=True) + epsilon)
            normed = (value * scale * gain).astype(bf16)
            taps[k, 1, pl.ds((r + 1) * pad, pad), :] = normed
            wide = normed.astype(f32)
            col_send[k, 0, pl.ds(r, 1), :] = wide[0:1]
            col_send[k, 1, pl.ds(r, 1), :] = wide[cols - 1 : cols]
        if k == 0:
            pl.semaphore_wait(barrier, 8)
        routes = [
            (taps.at[k, 1, pl.ds(pad, pad)], row_recv.at[k, 1]),
            (taps.at[k, 1, pl.ds(rows * pad, pad)], row_recv.at[k, 0]),
            (col_send.at[k, 0], col_recv.at[k, 1]),
            (col_send.at[k, 1], col_recv.at[k, 0]),
            (col_send.at[k, 0, pl.ds(0, 8)], corners.at[k, 0]),
            (col_send.at[k, 0, pl.ds(col_rows - 8, 8)], corners.at[k, 1]),
            (col_send.at[k, 1, pl.ds(0, 8)], corners.at[k, 2]),
            (col_send.at[k, 1, pl.ds(col_rows - 8, 8)], corners.at[k, 3]),
        ]
        copies = []
        for n, (source, target) in enumerate(routes):
            copies.append(
                pltpu.make_async_remote_copy(
                    src_ref=source, dst_ref=target,
                    send_sem=send_sem.at[k, n], recv_sem=recv_sem.at[k, n],
                    device_id=around[n], device_id_type=MESH,
                )
            )
            copies[-1].start()
        loads[k].wait()
        for copy in copies:
            copy.wait()

        def place(line, wide, before, after):
            at = pl.ds(line * pad, pad)
            left = jnp.where(spot == 0, before, pltpu.roll(wide, 1, 0))
            right = jnp.where(spot == cols - 1, after, pltpu.roll(wide, pad - 1, 0))
            taps[k, 0, at, :] = left.astype(bf16)
            taps[k, 2, at, :] = right.astype(bf16)

        for r in range(rows):
            place(
                r + 1, taps[k, 1, pl.ds((r + 1) * pad, pad), :].astype(f32),
                col_recv[k, 0, pl.ds(r, 1), :], col_recv[k, 1, pl.ds(r, 1), :],
            )
        low = rows - 1 - (col_rows - 8)
        for side, line, inside, west_at, east_at, row in (
            (0, 0, lat > 0, 3, 1, low),
            (1, rows + 1, lat < lat_parts - 1, 2, 0, 0),
        ):
            wide = jnp.where(inside, row_recv[k, side].astype(f32), 0.0)
            taps[k, 1, pl.ds(line * pad, pad), :] = wide.astype(bf16)
            place(
                line, wide,
                jnp.where(inside, corners[k, west_at, pl.ds(row, 1), :], 0.0),
                jnp.where(inside, corners[k, east_at, pl.ds(row, 1), :], 0.0),
            )
        total = jnp.zeros((rows * pad, channels), f32)
        for a in range(3):
            for b in range(3):
                total = total + jnp.dot(
                    taps[k, b, pl.ds(a * pad, rows * pad), :], weights[k, a, b],
                    preferred_element_type=f32,
                )
        fresh = state[...].reshape(rows * pad, channels) + gelu(total)
        if k == 0:
            state[...] = fresh.reshape(rows, pad, channels)
        else:
            for r in range(rows):
                piece = fresh[r * pad : (r + 1) * pad]
                out_ref[r] = piece[:cols]
                flat_ref[:, pl.ds(r * channels, channels)] = jnp.where(
                    spot < cols, piece, 0.0
                ).astype(bf16)
    tail = flat_ref.shape[1] - rows * channels
    if tail:
        flat_ref[:, pl.ds(rows * channels, tail)] = jnp.zeros((pad, tail), bf16)


def spectral_kernel(
    lat_parts, lon_parts, chunk, mode_pad,
    flat_ref, x_ref, keep_ref, fwd_ref, inv_ref, seed_ref, line_ref, fw_hbm, out_ref,
    columns, spec_out, spec_in, lat_spec, lat_filt, syn_out, syn_in, phys_out, phys_in,
    basis, fw, fw_sem, lon_send, lon_recv, lat_send, lat_recv,
):
    rows, cols, channels = x_ref.shape
    pad = flat_ref.shape[0]
    degrees = fw.shape[0]
    total_rows = rows * lat_parts
    total_degrees = degrees * lat_parts
    tiles = channels // LANES
    per = chunk // LANES
    lat, lon = lax.axis_index("lat"), lax.axis_index("lon")
    load = pltpu.make_async_copy(fw_hbm, fw, fw_sem)
    load.start()
    barrier = pltpu.get_barrier_semaphore()
    lon_peers = [lax.rem(lon + s, lon_parts) for s in range(1, lon_parts)]
    lat_peers = [lax.rem(lat + s, lat_parts) for s in range(1, lat_parts)]
    for peer in lon_peers:
        pl.semaphore_signal(barrier, inc=1, device_id=(lat, peer), device_id_type=MESH)
    for peer in lat_peers:
        pl.semaphore_signal(barrier, inc=1, device_id=(peer, lon), device_id_type=MESH)
    pl.semaphore_wait(barrier, lon_parts + lat_parts - 2)

    def scatter(phase, source_of, target):
        copies = []
        for s, peer in enumerate(lon_peers):
            copies.append(
                pltpu.make_async_remote_copy(
                    src_ref=source_of(peer), dst_ref=target.at[lon],
                    send_sem=lon_send.at[phase, s], recv_sem=lon_recv.at[phase, s],
                    device_id=(lat, peer), device_id_type=MESH,
                )
            )
            copies[-1].start()
        return copies

    def spread(phase, buffer):
        copies = []
        for s, peer in enumerate(lat_peers):
            copies.append(
                pltpu.make_async_remote_copy(
                    src_ref=buffer.at[lat], dst_ref=buffer.at[lat],
                    send_sem=lat_send.at[phase, s], recv_sem=lat_recv.at[phase, s],
                    device_id=(peer, lon), device_id_type=MESH,
                )
            )
            copies[-1].start()
        return copies

    def finish(copies):
        for copy in copies:
            copy.wait()

    def lane_block(part):
        return pl.ds(pl.multiple_of(part * chunk, LANES), chunk)

    def both(table, data):
        first = jnp.dot(table[0], data, preferred_element_type=f32)
        return first + jnp.dot(table[1], data, preferred_element_type=f32)

    copies = scatter(0, lambda peer: flat_ref.at[:, lane_block(peer)], columns)
    columns[lon] = flat_ref[:, lane_block(lon)]

    seeds = seed_ref[lon]
    growth = seeds[:, :total_degrees]
    damping = seeds[:, total_degrees : 2 * total_degrees]
    start = seeds[:, 2 * total_degrees : 3 * total_degrees]
    sectoral = seeds[:, 3 * total_degrees :]
    cosine = line_ref[0:1, :]
    before = jnp.zeros((mode_pad, total_rows), f32)
    latest = before
    for l in range(total_degrees):
        grown = growth[:, l : l + 1] * (cosine * latest - damping[:, l : l + 1] * before)
        before, latest = latest, grown + start[:, l : l + 1] * sectoral
        basis[pl.ds(l * mode_pad, mode_pad), :] = latest

    def expand(values, first_row, lines):
        wide = lines * mode_pad
        row = lax.broadcasted_iota(jnp.int32, (total_rows, wide), 0)
        column = lax.broadcasted_iota(jnp.int32, (total_rows, wide), 1)
        low = row * mode_pad
        at = column + first_row * mode_pad
        pick = jnp.where((at >= low) & (at < low + mode_pad), 1.0, 0.0).astype(bf16)
        upper = values.astype(bf16)
        lower = (values - upper.astype(f32)).astype(bf16)
        shape = (values.shape[0], wide)
        own = lax.rem(lax.broadcasted_iota(jnp.int32, shape, 0), mode_pad)
        other = lax.rem(lax.broadcasted_iota(jnp.int32, shape, 1), mode_pad)
        same = own == other
        return [
            jnp.where(same, jnp.dot(part, pick, preferred_element_type=f32), 0.0).astype(bf16)
            for part in (upper, lower)
        ]

    own_rows = pl.ds(pl.multiple_of(lat * degrees * mode_pad, 16), degrees * mode_pad)
    analysis = expand(basis[own_rows, :] * line_ref[1:2, :], 0, total_rows)
    rebuild = expand(basis[...], lat * rows, rows)

    finish(copies)
    spectrum = both(fwd_ref, columns[...].reshape(lon_parts * pad, chunk))
    spec_out[...] = spectrum.astype(bf16).reshape(spec_out.shape)
    copies = scatter(1, lambda peer: spec_out.at[peer], spec_in)
    spec_in[lon] = spec_out[lon]
    finish(copies)
    for i in range(rows):
        for c in range(tiles):
            part, tile = divmod(i * tiles + c, per)
            lat_spec[lat, pl.ds(i * mode_pad, mode_pad), pl.ds(c * LANES, LANES)] = spec_in[
                part, :, pl.ds(tile * LANES, LANES)
            ]
    finish(spread(0, lat_spec))
    coefficients = both(
        analysis, lat_spec[...].reshape(total_rows * mode_pad, channels)
    ).astype(bf16)
    load.wait()
    for l in range(degrees):
        at = pl.ds(l * mode_pad, mode_pad)
        mixed = jnp.dot(
            coefficients[l * mode_pad : (l + 1) * mode_pad], fw[l], preferred_element_type=f32
        )
        lat_filt[lat, at, :] = (mixed * keep_ref[at, :]).astype(bf16)
    finish(spread(1, lat_filt))
    filtered = lat_filt[...].reshape(total_degrees * mode_pad, channels)
    over = (((0,), (0,)), ((), ()))
    synthesis = sum(
        lax.dot_general(part, filtered, over, preferred_element_type=f32) for part in rebuild
    ).astype(bf16)
    syn_out[...] = jnp.zeros(syn_out.shape, bf16)
    for i in range(rows):
        for c in range(tiles):
            part, tile = divmod(i * tiles + c, per)
            syn_out[part, :, pl.ds(tile * LANES, LANES)] = synthesis[
                i * mode_pad : (i + 1) * mode_pad, c * LANES : (c + 1) * LANES
            ]
    copies = scatter(2, lambda peer: syn_out.at[peer], syn_in)
    syn_in[lon] = syn_out[lon]
    finish(copies)
    physical = both(inv_ref, syn_in[...].reshape(lon_parts * mode_pad, chunk))
    phys_out[...] = physical.astype(bf16).reshape(phys_out.shape)
    copies = scatter(3, lambda peer: phys_out.at[peer], phys_in)
    phys_in[lon] = phys_out[lon]
    finish(copies)
    for i in range(rows):
        for c in range(tiles):
            part, tile = divmod(i * tiles + c, per)
            at = pl.ds(c * LANES, LANES)
            value = phys_in[part, :, pl.ds(tile * LANES, LANES)].astype(f32)
            out_ref[i, :, at] = x_ref[i, :, at] + gelu(value)[:cols]


def per_device(grid_state, norm_gain, conv_weight, filter_weight, degree_keep):
    rows, cols, channels = grid_state.shape
    lat_parts, lon_parts = lax.axis_size("lat"), lax.axis_size("lon")
    degrees, orders = degree_keep.shape
    col_pad, mode_pad = up(cols, 16), up(2 * orders, 16)
    col_rows = up(rows, 8)
    chunk = up(-(-rows * channels // lon_parts), LANES)
    vmem = pl.BlockSpec(memory_space=pltpu.VMEM)
    hbm = pl.BlockSpec(memory_space=pl.ANY)
    dma = pltpu.SemaphoreType.DMA
    x, flat = pl.pallas_call(
        functools.partial(conv_kernel, lat_parts, lon_parts, chunk),
        out_shape=(
            jax.ShapeDtypeStruct((rows, cols, channels), f32),
            jax.ShapeDtypeStruct((col_pad, lon_parts * chunk), bf16),
        ),
        in_specs=[vmem, vmem, hbm],
        out_specs=(vmem, vmem),
        scratch_shapes=[
            pltpu.VMEM((rows, col_pad, channels), f32),
            pltpu.VMEM((2, 3, (rows + 2) * col_pad, channels), bf16),
            pltpu.VMEM((2, 3, 3, channels, channels), bf16),
            pltpu.VMEM((2, 2, col_rows, channels), f32),
            pltpu.VMEM((2, 2, col_rows, channels), f32),
            pltpu.VMEM((2, 2, col_pad, channels), bf16),
            pltpu.VMEM((2, 4, 8, channels), f32),
            dma((2,)),
            dma((2, 8)),
            dma((2, 8)),
        ],
        compiler_params=pltpu.CompilerParams(collective_id=0, has_side_effects=True),
        name="conv_pair",
    )(grid_state, norm_gain, conv_weight)

    forward, inverse = fourier_tables(lon_parts, cols, col_pad, orders, mode_pad)
    seeds, lines = legendre_seeds(
        lon_parts, orders, mode_pad, degrees * lat_parts, rows * lat_parts
    )
    keep = jnp.repeat(degree_keep.astype(f32), 2, axis=1)
    keep = jnp.pad(keep, ((0, 0), (0, mode_pad - 2 * orders))).reshape(degrees * mode_pad, 1)
    block = pltpu.VMEM((lon_parts, mode_pad, chunk), bf16)
    column_block = pltpu.VMEM((lon_parts, col_pad, chunk), bf16)
    return pl.pallas_call(
        functools.partial(spectral_kernel, lat_parts, lon_parts, chunk, mode_pad),
        out_shape=jax.ShapeDtypeStruct((rows, cols, channels), f32),
        in_specs=[vmem] * 7 + [hbm],
        out_specs=vmem,
        scratch_shapes=[
            column_block,
            block,
            block,
            pltpu.VMEM((lat_parts, rows * mode_pad, channels), bf16),
            pltpu.VMEM((lat_parts, degrees * mode_pad, channels), bf16),
            block,
            block,
            column_block,
            column_block,
            pltpu.VMEM((degrees * lat_parts * mode_pad, rows * lat_parts), f32),
            pltpu.VMEM((degrees, channels, channels), bf16),
            dma(()),
            dma((4, lon_parts - 1)),
            dma((4, lon_parts - 1)),
            dma((2, lat_parts - 1)),
            dma((2, lat_parts - 1)),
        ],
        compiler_params=pltpu.CompilerParams(collective_id=1, has_side_effects=True),
        name="spectral_block",
    )(
        flat, x, keep, jnp.asarray(forward), jnp.asarray(inverse),
        jnp.asarray(seeds), jnp.asarray(lines), filter_weight,
    )


def solution(mesh):
    in_specs = (P("lat", "lon", None), P(), P(), P("lat", None, None), P("lat", "lon"))
    out_specs = P("lat", "lon", None)
    return jax.shard_map(
        per_device, mesh=mesh, in_specs=in_specs, out_specs=out_specs, check_vma=False
    )
```

time: 432 us -> 65.3 us (0.15); the launches traced: 426 us -> 65 us
  other arithmetic: 142 us -> 0.69 us
  local copies, waits for them, and re-layouts: 140 us -> 2.56 us
  Pallas kernels: 0 us -> 61.7 us
  matrix products: 41.5 us -> 0 us
  blocking collectives: 32.7 us -> 0 us
  loops' own time: 31.1 us -> 0 us
  starting transfers between devices: 26.3 us -> 0 us
  waiting for transfers between devices: 11.3 us -> 0 us
    while x45 -> x0, other arithmetic: 62.3 us -> none
    pallas_call x0 -> x2, Pallas kernels: none -> 61.7 us  [the longest x1 42.1 us: per_device(): pl.pallas_call(functools.partial(spectral_kernel, lat_parts, lon_parts, c...]
    reshape x26 -> x2, local copies, waits for them, and re-layouts: 43.8 us -> 0.75 us  [the longest x1 0.74 us: per_device(): jnp.pad(keep, ((0, 0), (0, mode_pad - 2 * orders)))]
    dot_general x27 -> x0, matrix products: 41.5 us -> none  [the longest x18 29.2 us: conv_taps(): jnp.dot(window, weight[row_tap, col_tap], preferred_element_type=jnp.floa...]
    eq x48 -> x0, other arithmetic: 31.6 us -> none  [advance(): degree == order_i]
    another operation x1 -> x0, loops' own time: 31.1 us -> none  [legendre_table(): lax.scan(advance, (zero_rows, zero_rows), jnp.arange(amount, dtype=jnp.in...]
    unnamed x41 -> x2, local copies, waits for them, and re-layouts: 26.1 us -> 1.79 us
    mul x12 -> x0, local copies, waits for them, and re-layouts: 23.9 us -> none  [the longest x8 17.1 us: per_device(): return grid_state + jax.nn.gelu(physical.astype(f32), approximate=False)]
  transfers between devices with their start and end apart: 11 -> 0, of which waited for: 4 -> 0; matrix products, arithmetic and copies ran while one was open for 35% -> 0% of each run, Pallas kernels for 0% -> 0%
where the time goes in v1:
time: 65.3 us; the launch traced here: 65 us
  Pallas kernels  61.7 us (94%)
  local copies, waits for them, and re-layouts  2.56 us (4%)
  other arithmetic  0.69 us (1%)
    pallas_call x1, Pallas kernels, per_device(): pl.pallas_call(functools.partial(spectral_kernel, lat_parts, lon_parts, c...  42.1 us
    pallas_call x1, Pallas kernels, per_device(): pl.pallas_call(functools.partial(conv_kernel, lat_parts, lon_parts, chunk...  19.6 us
    unnamed x2, local copies, waits for them, and re-layouts  1.79 us

profile of v1, /device:TPU:0, one launch (start us, length us, event | category | flops | bytes accessed | tf_op | source)
XLA Modules:
  0.0 65.0 jit_solution(5215133048571046765)
XLA Ops:
  0.0 0.7 %convert_element_type.5 = f32[12,6]{0,1:T(8,128)S(1)} convert(s32[12,6]{0,1:T(8,128)} %param.13) | non-fusion elementwise | flops 72 | bytes 576 | tf_op jit(solution)/shard_map/convert_element_type | solution.py:379
  0.7 0.1 copy.13
  0.8 0.7 %reshape.8.keep_ref = f32[192,1]{1,0:T(8,128)} reshape(f32[12,16]{1,0:T(8,128)S(1)} %pad.4.clone) | data formatting | bytes 1536 | tf_op jit(solution)/shard_map/reshape | solution.py:380
  1.6 19.6 %conv_pair.1 = (f32[12,15,384]{2,1,0:T(8,128)}, bf16[16,5120]{1,0:T(8,128)(2,1)}) custom-call(f32[12,15,384]{2,1,0:T(8,128)} %x_ref.1, f32[2,384]{1,0:T(2,128)} %gain_ref.1, bf16[2,3,3,384,384]{4,3,2,1,0:T(8,128)(2,1)} %w_hbm.1), custom_call_target="tpu_custom_call" | custom-call | tf_op jit(solution)/shard_map/conv_pair/pallas_call | solution.py:351
  21.2 42.1 %spectral_block.1 = f32[12,15,384]{2,1,0:T(8,128)} custom-call(bf16[16,5120]{1,0:T(8,128)(2,1)} %get-tuple-element.7.flat_ref, f32[12,15,384]{2,1,0:T(8,128)} %get-tuple-element.8.x_ref, f32[192,1]{1,0:T(8,128)} %reshape.8.keep_ref, bf16[2,128,128]{2,1,0:T(8,128)(2,1)} %constant.11.clone.fwd_ref, bf16[2,128,128]{2,1,0:T(8,128)(2,1)} %constant.12.clone.inv_ref, ...), custom_call_target="tpu_custom_call" | custom-call | tf_op jit(solution)/shard_map/spectral_block/pallas_call | solution.py:383
  63.3 1.7 %copy.15 = f32[12,15,384]{2,1,0:T(8,128)} copy(f32[12,15,384]{2,1,0:T(8,128)} %spectral_block.1) | data formatting | bytes 552960
  (3 shorter events, 0.0 us)

commit v2 on v1

v2 whole, which is shorter than its diff:
```python
import functools
import math

import jax
import jax.numpy as jnp
import ml_dtypes
import numpy as np
from jax import lax
from jax.experimental import pallas as pl
from jax.experimental.pallas import tpu as pltpu
from jax.sharding import PartitionSpec as P

epsilon = 1e-06
LANES = 128
MESH = pl.DeviceIdType.MESH
f32 = jnp.float32
bf16 = jnp.bfloat16


def up(value, step):
    return -(-value // step) * step


def gelu(value):
    return 0.5 * value * (1.0 + lax.erf(value * math.sqrt(0.5)))


def split(table):
    upper = table.astype(ml_dtypes.bfloat16)
    lower = (table - upper.astype(np.float64)).astype(ml_dtypes.bfloat16)
    return np.stack([upper, lower])


def fourier_tables(lon_parts, cols, col_pad, orders, mode_pad):
    total = lon_parts * cols
    forward = np.zeros((lon_parts, mode_pad, lon_parts, col_pad))
    inverse = np.zeros((lon_parts, col_pad, lon_parts, mode_pad))
    m = np.arange(lon_parts * orders)[:, None]
    j = np.arange(total)[None, :]
    phase = (m * j % total) * (2.0 * math.pi / total)
    pair = np.stack([np.cos(phase), -np.sin(phase)], axis=1)
    pair = pair.reshape(lon_parts, 2 * orders, lon_parts, cols)
    weight = np.where(m == 0, 1.0, 2.0)[:, :, None]
    back = (np.stack([np.cos(phase), -np.sin(phase)], axis=1) * weight).reshape(pair.shape)
    forward[:, : 2 * orders, :, :cols] = pair * (2.0 * math.pi / total)
    inverse[:, :cols, :, : 2 * orders] = back.transpose(2, 3, 0, 1)
    side_m, side_c = lon_parts * mode_pad, lon_parts * col_pad
    return split(forward.reshape(side_m, side_c)), split(inverse.reshape(side_c, side_m))


def legendre_seeds(lon_parts, orders, mode_pad, degrees, rows):
    count = lon_parts * orders
    m = np.arange(count, dtype=np.float64)[:, None]
    l = np.arange(degrees, dtype=np.float64)[None, :]
    theta = (np.arange(rows) + 0.5) * (math.pi / rows)
    gammas = np.array([math.lgamma(v + 0.5) - math.lgamma(v + 1.0) for v in range(count)])
    log_start = 0.5 * (
        np.log((2.0 * m + 1.0) / (4.0 * math.pi)) + gammas[:, None] - 0.5 * math.log(math.pi)
    ) + m * np.log(np.sin(theta))[None, :]
    growth = np.where(
        l > m, np.sqrt(np.maximum(4 * l * l - 1, 1) / np.maximum(l * l - m * m, 1)), 0.0
    )
    prior = l - 1.0
    damping = np.sqrt(
        np.maximum(prior * prior - m * m, 0) / np.maximum(4 * prior * prior - 1, 1)
    )
    table = np.concatenate([growth, damping, (l == m) * 1.0, np.exp(log_start)], axis=1)
    table = np.repeat(table.reshape(lon_parts, orders, -1), 2, axis=1)
    full = np.zeros((lon_parts, up(mode_pad, 8), table.shape[2]), np.float32)
    full[:, : 2 * orders] = table
    lines = np.stack([np.cos(theta), np.sin(theta) * (math.pi / rows)]).astype(np.float32)
    return full, np.concatenate([lines, np.zeros((6, rows), np.float32)])


def block_kernel(
    lat_parts, lon_parts, chunk, modes,
    x_ref, gain_ref, keep_ref, fwd_ref, inv_ref, seed_ref, line_ref, w_hbm, fw_hbm, out_ref,
    state, taps, weights, col_send, col_recv, row_recv, corners, flat,
    columns, spec_out, spec_in, lat_spec, lat_filt, syn_out, syn_in, phys_out, phys_in,
    basis, analysis, rebuild, packed, fw,
    w_sem, fw_sem, send_sem, recv_sem, lon_send, lon_recv, lat_send, lat_recv,
):
    rows, cols, channels = x_ref.shape
    pad = state.shape[1]
    mode_pad = spec_in.shape[1]
    col_rows = col_send.shape[2]
    degrees = fw.shape[0]
    total_rows = rows * lat_parts
    total_degrees = degrees * lat_parts
    tiles = channels // LANES
    per = chunk // LANES
    lat, lon = lax.axis_index("lat"), lax.axis_index("lon")
    loads = [
        pltpu.make_async_copy(w_hbm.at[k], weights.at[k], w_sem.at[k]) for k in range(2)
    ]
    loads.append(pltpu.make_async_copy(fw_hbm, fw, fw_sem))
    for load in loads:
        load.start()
    north = lax.rem(lat + lat_parts - 1, lat_parts)
    south = lax.rem(lat + 1, lat_parts)
    west = lax.rem(lon + lon_parts - 1, lon_parts)
    east = lax.rem(lon + 1, lon_parts)
    lon_peers = [lax.rem(lon + s, lon_parts) for s in range(1, lon_parts)]
    lat_peers = [lax.rem(lat + s, lat_parts) for s in range(1, lat_parts)]
    corner_peers = [(north, west), (south, west), (north, east), (south, east)]
    around = [(north, lon), (south, lon), (lat, west), (lat, east)] + corner_peers
    greeted = [(lat, peer) for peer in lon_peers] + [(peer, lon) for peer in lat_peers]
    greeted += corner_peers
    barrier = pltpu.get_barrier_semaphore()
    for device in greeted:
        pl.semaphore_signal(barrier, inc=1, device_id=device, device_id_type=MESH)
    spot = lax.broadcasted_iota(jnp.int32, (pad, channels), 0)
    for r in range(rows):
        state[r, pl.ds(cols, pad - cols), :] = jnp.zeros((pad - cols, channels), f32)
        state[r, pl.ds(0, cols), :] = x_ref[r]
    col_send[...] = jnp.zeros(col_send.shape, f32)

    def legendre():
        seeds = seed_ref[lon]
        growth = seeds[:, :total_degrees]
        damping = seeds[:, total_degrees : 2 * total_degrees]
        start = seeds[:, 2 * total_degrees : 3 * total_degrees]
        sectoral = seeds[:, 3 * total_degrees :]
        cosine = line_ref[0:1, :]
        before = jnp.zeros(sectoral.shape, f32)
        latest = before
        for l in range(total_degrees):
            grown = growth[:, l : l + 1] * (cosine * latest - damping[:, l : l + 1] * before)
            before, latest = latest, grown + start[:, l : l + 1] * sectoral
            basis[pl.ds(l * modes, modes), :] = latest[:modes]

    def expand(values, first_row, target):
        shape = target.shape[1:]
        row = lax.broadcasted_iota(jnp.int32, (total_rows, shape[1]), 0) * modes
        at = lax.broadcasted_iota(jnp.int32, (total_rows, shape[1]), 1) + first_row * modes
        pick = jnp.where((at >= row) & (at < row + modes), 1.0, 0.0).astype(bf16)
        upper = values.astype(bf16)
        lower = (values - upper.astype(f32)).astype(bf16)
        own = lax.rem(lax.broadcasted_iota(jnp.int32, shape, 0), modes)
        other = lax.rem(lax.broadcasted_iota(jnp.int32, shape, 1), modes)
        same = own == other
        for n, part in enumerate((upper, lower)):
            wide = jnp.dot(part, pick, preferred_element_type=f32)
            target[n] = jnp.where(same, wide, 0.0).astype(bf16)

    def place(k, line, wide, before, after):
        at = pl.ds(line * pad, pad)
        left = jnp.where(spot == 0, before, pltpu.roll(wide, 1, 0))
        right = jnp.where(spot == cols - 1, after, pltpu.roll(wide, pad - 1, 0))
        taps[k, 0, at, :] = left.astype(bf16)
        taps[k, 2, at, :] = right.astype(bf16)

    for k in range(2):
        gain = gain_ref[k : k + 1, :]
        for r in range(rows):
            value = state[r]
            scale = lax.rsqrt(jnp.mean(value * value, axis=-1, keepdims=True) + epsilon)
            normed = (value * scale * gain).astype(bf16)
            taps[k, 1, pl.ds((r + 1) * pad, pad), :] = normed
            wide = normed.astype(f32)
            col_send[k, 0, pl.ds(r, 1), :] = wide[0:1]
            col_send[k, 1, pl.ds(r, 1), :] = wide[cols - 1 : cols]
        if k == 0:
            pl.semaphore_wait(barrier, len(greeted))
        routes = [
            (taps.at[k, 1, pl.ds(pad, pad)], row_recv.at[k, 1]),
            (taps.at[k, 1, pl.ds(rows * pad, pad)], row_recv.at[k, 0]),
            (col_send.at[k, 0], col_recv.at[k, 1]),
            (col_send.at[k, 1], col_recv.at[k, 0]),
            (col_send.at[k, 0, pl.ds(0, 8)], corners.at[k, 0]),
            (col_send.at[k, 0, pl.ds(col_rows - 8, 8)], corners.at[k, 1]),
            (col_send.at[k, 1, pl.ds(0, 8)], corners.at[k, 2]),
            (col_send.at[k, 1, pl.ds(col_rows - 8, 8)], corners.at[k, 3]),
        ]
        copies = []
        for n, (source, target) in enumerate(routes):
            copies.append(
                pltpu.make_async_remote_copy(
                    src_ref=source, dst_ref=target,
                    send_sem=send_sem.at[k, n], recv_sem=recv_sem.at[k, n],
                    device_id=around[n], device_id_type=MESH,
                )
            )
        for n in (4, 5, 6, 7, 0, 1, 2, 3):
            copies[n].start()
        if k == 0:
            legendre()
            own_rows = pl.ds(pl.multiple_of(lat * degrees * modes, 8), degrees * modes)
            expand(basis[own_rows, :] * line_ref[1:2, :], 0, analysis)
        else:
            expand(basis[...], lat * rows, rebuild)
        loads[k].wait()
        for copy in copies:
            copy.wait()
        for r in range(rows):
            place(
                k, r + 1, taps[k, 1, pl.ds((r + 1) * pad, pad), :].astype(f32),
                col_recv[k, 0, pl.ds(r, 1), :], col_recv[k, 1, pl.ds(r, 1), :],
            )
        low = rows - 1 - (col_rows - 8)
        for side, line, inside, west_at, east_at, row in (
            (0, 0, lat > 0, 3, 1, low),
            (1, rows + 1, lat < lat_parts - 1, 2, 0, 0),
        ):
            wide = jnp.where(inside, row_recv[k, side].astype(f32), 0.0)
            taps[k, 1, pl.ds(line * pad, pad), :] = wide.astype(bf16)
            place(
                k, line, wide,
                jnp.where(inside, corners[k, west_at, pl.ds(row, 1), :], 0.0),
                jnp.where(inside, corners[k, east_at, pl.ds(row, 1), :], 0.0),
            )
        total = jnp.zeros((rows * pad, channels), f32)
        for a in range(3):
            for b in range(3):
                total = total + jnp.dot(
                    taps[k, b, pl.ds(a * pad, rows * pad), :], weights[k, a, b],
                    preferred_element_type=f32,
                )
        fresh = state[...].reshape(rows * pad, channels) + gelu(total)
        state[...] = fresh.reshape(rows, pad, channels)
    for r in range(rows):
        flat[:, pl.ds(r * channels, channels)] = jnp.where(
            spot < cols, state[r], 0.0
        ).astype(bf16)
    tail = flat.shape[1] - rows * channels
    if tail:
        flat[:, pl.ds(rows * channels, tail)] = jnp.zeros((pad, tail), bf16)

    def scatter(phase, source_of, target):
        copies = []
        for s, peer in enumerate(lon_peers):
            copies.append(
                pltpu.make_async_remote_copy(
                    src_ref=source_of(peer), dst_ref=target.at[lon],
                    send_sem=lon_send.at[phase, s], recv_sem=lon_recv.at[phase, s],
                    device_id=(lat, peer), device_id_type=MESH,
                )
            )
            copies[-1].start()
        return copies

    def spread(phase, buffer):
        copies = []
        for s, peer in enumerate(lat_peers):
            copies.append(
                pltpu.make_async_remote_copy(
                    src_ref=buffer.at[lat], dst_ref=buffer.at[lat],
                    send_sem=lat_send.at[phase, s], recv_sem=lat_recv.at[phase, s],
                    device_id=(peer, lon), device_id_type=MESH,
                )
            )
            copies[-1].start()
        return copies

    def finish(copies):
        for copy in copies:
            copy.wait()

    def lane_block(part):
        return pl.ds(pl.multiple_of(part * chunk, LANES), chunk)

    def both(table, data):
        first = jnp.dot(table[0], data, preferred_element_type=f32)
        return first + jnp.dot(table[1], data, preferred_element_type=f32)

    copies = scatter(0, lambda peer: flat.at[:, lane_block(peer)], columns)
    columns[lon] = flat[:, lane_block(lon)]
    finish(copies)
    spectrum = both(fwd_ref, columns[...].reshape(lon_parts * pad, chunk))
    spec_out[...] = spectrum.astype(bf16).reshape(spec_out.shape)
    copies = scatter(1, lambda peer: spec_out.at[peer], spec_in)
    spec_in[lon] = spec_out[lon]
    finish(copies)
    for i in range(rows):
        for c in range(tiles):
            part, tile = divmod(i * tiles + c, per)
            piece = spec_in[part, :, pl.ds(tile * LANES, LANES)].astype(f32)
            packed[pl.ds(i * modes, modes), pl.ds(c * LANES, LANES)] = piece[:modes]
    lat_spec[lat] = packed[pl.ds(0, rows * modes), :].astype(bf16)
    finish(spread(0, lat_spec))
    coefficients = both(analysis, lat_spec[...].reshape(total_rows * modes, channels))
    loads[2].wait()
    shape = (modes, keep_ref.shape[1])
    order = 2 * lax.broadcasted_iota(jnp.int32, shape, 1)
    mode = lax.broadcasted_iota(jnp.int32, shape, 0)
    mine = (mode >= order) & (mode < order + 2)
    for l in range(degrees):
        kept = jnp.where(mine, keep_ref[l : l + 1, :].astype(f32), 0.0)
        mixed = jnp.dot(
            coefficients[l * modes : (l + 1) * modes].astype(bf16), fw[l],
            preferred_element_type=f32,
        )
        packed[pl.ds(l * modes, modes), :] = mixed * jnp.sum(kept, axis=1, keepdims=True)
    lat_filt[lat] = packed[pl.ds(0, degrees * modes), :].astype(bf16)
    finish(spread(1, lat_filt))
    filtered = lat_filt[...].reshape(total_degrees * modes, channels)
    over = (((0,), (0,)), ((), ()))
    packed[pl.ds(0, rows * modes), :] = sum(
        lax.dot_general(rebuild[n], filtered, over, preferred_element_type=f32)
        for n in range(2)
    )
    packed[pl.ds(rows * modes, mode_pad), :] = jnp.zeros((mode_pad, channels), f32)
    syn_out[...] = jnp.zeros(syn_out.shape, bf16)
    for i in range(rows):
        for c in range(tiles):
            part, tile = divmod(i * tiles + c, per)
            syn_out[part, :, pl.ds(tile * LANES, LANES)] = packed[
                pl.ds(i * modes, mode_pad), pl.ds(c * LANES, LANES)
            ].astype(bf16)
    copies = scatter(2, lambda peer: syn_out.at[peer], syn_in)
    syn_in[lon] = syn_out[lon]
    finish(copies)
    physical = both(inv_ref, syn_in[...].reshape(lon_parts * mode_pad, chunk))
    phys_out[...] = physical.astype(bf16).reshape(phys_out.shape)
    copies = scatter(3, lambda peer: phys_out.at[peer], phys_in)
    phys_in[lon] = phys_out[lon]
    finish(copies)
    for i in range(rows):
        for c in range(tiles):
            part, tile = divmod(i * tiles + c, per)
            at = pl.ds(c * LANES, LANES)
            value = phys_in[part, :, pl.ds(tile * LANES, LANES)].astype(f32)
            out_ref[i, :, at] = (state[i, :, at] + gelu(value))[:cols]


def per_device(grid_state, norm_gain, conv_weight, filter_weight, degree_keep):
    rows, cols, channels = grid_state.shape
    lat_parts, lon_parts = lax.axis_size("lat"), lax.axis_size("lon")
    degrees, orders = degree_keep.shape
    modes = 2 * orders
    col_pad, mode_pad = up(cols, 16), up(modes, 16)
    col_rows = up(rows, 8)
    chunk = up(-(-rows * channels // lon_parts), LANES)
    total_rows, total_degrees = rows * lat_parts, degrees * lat_parts
    vmem = pl.BlockSpec(memory_space=pltpu.VMEM)
    hbm = pl.BlockSpec(memory_space=pl.ANY)
    dma = pltpu.SemaphoreType.DMA
    forward, inverse = fourier_tables(lon_parts, cols, col_pad, orders, mode_pad)
    seeds, lines = legendre_seeds(lon_parts, orders, modes, total_degrees, total_rows)
    block = pltpu.VMEM((lon_parts, mode_pad, chunk), bf16)
    column_block = pltpu.VMEM((lon_parts, col_pad, chunk), bf16)
    return pl.pallas_call(
        functools.partial(block_kernel, lat_parts, lon_parts, chunk, modes),
        out_shape=jax.ShapeDtypeStruct((rows, cols, channels), f32),
        in_specs=[vmem] * 7 + [hbm, hbm],
        out_specs=vmem,
        scratch_shapes=[
            pltpu.VMEM((rows, col_pad, channels), f32),
            pltpu.VMEM((2, 3, (rows + 2) * col_pad, channels), bf16),
            pltpu.VMEM((2, 3, 3, channels, channels), bf16),
            pltpu.VMEM((2, 2, col_rows, channels), f32),
            pltpu.VMEM((2, 2, col_rows, channels), f32),
            pltpu.VMEM((2, 2, col_pad, channels), bf16),
            pltpu.VMEM((2, 4, 8, channels), f32),
            pltpu.VMEM((col_pad, lon_parts * chunk), bf16),
            column_block,
            block,
            block,
            pltpu.VMEM((lat_parts, rows * modes, channels), bf16),
            pltpu.VMEM((lat_parts, degrees * modes, channels), bf16),
            block,
            block,
            column_block,
            column_block,
            pltpu.VMEM((total_degrees * modes, total_rows), f32),
            pltpu.VMEM((2, degrees * modes, total_rows * modes), bf16),
            pltpu.VMEM((2, total_degrees * modes, rows * modes), bf16),
            pltpu.VMEM((max(rows, degrees) * modes + mode_pad, channels), f32),
            pltpu.VMEM((degrees, channels, channels), bf16),
            dma((2,)),
            dma(()),
            dma((2, 8)),
            dma((2, 8)),
            dma((4, lon_parts - 1)),
            dma((4, lon_parts - 1)),
            dma((2, lat_parts - 1)),
            dma((2, lat_parts - 1)),
        ],
        compiler_params=pltpu.CompilerParams(collective_id=0, has_side_effects=True),
        name="block",
    )(
        grid_state, norm_gain, degree_keep, jnp.asarray(forward), jnp.asarray(inverse),
        jnp.asarray(seeds), jnp.asarray(lines), conv_weight, filter_weight,
    )


def solution(mesh):
    in_specs = (P("lat", "lon", None), P(), P(), P("lat", None, None), P("lat", "lon"))
    out_specs = P("lat", "lon", None)
    return jax.shard_map(
        per_device, mesh=mesh, in_specs=in_specs, out_specs=out_specs, check_vma=False
    )
```

time: 65.3 us -> 57.1 us (0.87)
  Pallas kernels: 61.7 us -> 53.9 us
  other arithmetic: 0.69 us -> 0 us
    pallas_call x2 -> x1, Pallas kernels: 61.7 us -> 53.9 us  [per_device(): pl.pallas_call(functools.partial(block_kernel, lat_parts, lon_parts, chun...]
    unnamed x2, local copies, waits for them, and re-layouts: 1.79 us -> 3.06 us
    reshape x2 -> x0, local copies, waits for them, and re-layouts: 0.75 us -> none  [the longest x1 0.74 us: per_device(): jnp.pad(keep, ((0, 0), (0, mode_pad - 2 * orders)))]
    convert_element_type x1 -> x0, other arithmetic: 0.69 us -> none  [per_device(): keep = jnp.repeat(degree_keep.astype(f32), 2, axis=1)]
where the time goes in v2:
time: 57.1 us; the launch traced here: 56.9 us
  Pallas kernels  53.9 us (94%)
  local copies, waits for them, and re-layouts  3.06 us (5%)
    pallas_call x1, Pallas kernels, per_device(): pl.pallas_call(functools.partial(block_kernel, lat_parts, lon_parts, chun...  53.9 us
    unnamed x2, local copies, waits for them, and re-layouts  3.06 us

profile of v2, /device:TPU:0, one launch (start us, length us, event | category | flops | bytes accessed | tf_op | source)
XLA Modules:
  0.0 56.9 jit_solution(17406185105664716949)
XLA Ops:
  0.0 1.4 %copy.10.keep_ref = s32[12,6]{1,0:T(8,128)} copy(s32[12,6]{0,1:T(8,128)} %param.13) | data formatting | bytes 576 | tf_op args[4]
  1.4 53.9 %block.1 = f32[12,15,384]{2,1,0:T(8,128)} custom-call(f32[12,15,384]{2,1,0:T(8,128)} %x_ref.1, f32[2,384]{1,0:T(2,128)} %gain_ref.1, s32[12,6]{1,0:T(8,128)} %copy.10.keep_ref, bf16[2,128,128]{2,1,0:T(8,128)(2,1)} %constant.8.clone.fwd_ref, bf16[2,128,128]{2,1,0:T(8,128)(2,1)} %constant.9.clone.inv_ref, f32[8,16,192]{2,1,0:T(8,128)} %constant.10.clone.seed_ref, ...), custom_call_target="tpu_custom_call" | custom-call | tf_op jit(solution)/shard_map/block/pallas_call | solution.py:342
  55.2 1.7 %copy.12 = f32[12,15,384]{2,1,0:T(8,128)} copy(f32[12,15,384]{2,1,0:T(8,128)} %block.1) | data formatting | bytes 552960

commit v3 on v2

--- a/solution.py
+++ b/solution.py
@@ -73,22 +73,20 @@
 
 
 def block_kernel(
-    lat_parts, lon_parts, chunk, modes,
+    lat_parts, lon_parts, groups, modes,
     x_ref, gain_ref, keep_ref, fwd_ref, inv_ref, seed_ref, line_ref, w_hbm, fw_hbm, out_ref,
     state, taps, weights, col_send, col_recv, row_recv, corners, flat,
     columns, spec_out, spec_in, lat_spec, lat_filt, syn_out, syn_in, phys_out, phys_in,
-    basis, analysis, rebuild, packed, fw,
+    basis, analysis, rebuild, packed, mixed, fw,
     w_sem, fw_sem, send_sem, recv_sem, lon_send, lon_recv, lat_send, lat_recv,
 ):
     rows, cols, channels = x_ref.shape
     pad = state.shape[1]
-    mode_pad = spec_in.shape[1]
+    mode_pad = spec_in[0].shape[1]
     col_rows = col_send.shape[2]
     degrees = fw.shape[0]
     total_rows = rows * lat_parts
     total_degrees = degrees * lat_parts
-    tiles = channels // LANES
-    per = chunk // LANES
     lat, lon = lax.axis_index("lat"), lax.axis_index("lon")
     loads = [
         pltpu.make_async_copy(w_hbm.at[k], weights.at[k], w_sem.at[k]) for k in range(2)
@@ -218,34 +216,42 @@
                 )
         fresh = state[...].reshape(rows * pad, channels) + gelu(total)
         state[...] = fresh.reshape(rows, pad, channels)
-    for r in range(rows):
-        flat[:, pl.ds(r * channels, channels)] = jnp.where(
-            spot < cols, state[r], 0.0
-        ).astype(bf16)
-    tail = flat.shape[1] - rows * channels
-    if tail:
-        flat[:, pl.ds(rows * channels, tail)] = jnp.zeros((pad, tail), bf16)
-
-    def scatter(phase, source_of, target):
+
+    def cells(g):
+        first, last, per = groups[g]
+        for i in range(rows):
+            for c in range(first, last):
+                part, tile = divmod(i * (last - first) + c - first, per)
+                yield i, c, part, pl.ds(tile * LANES, LANES)
+
+    def width(g):
+        first, last, per = groups[g]
+        return pl.ds(first * LANES, (last - first) * LANES)
+
+    def chunk(g, part):
+        size = groups[g][2] * LANES
+        return pl.ds(pl.multiple_of(part * size, LANES), size)
+
+    def scatter(phase, g, source_of, target):
         copies = []
         for s, peer in enumerate(lon_peers):
             copies.append(
                 pltpu.make_async_remote_copy(
                     src_ref=source_of(peer), dst_ref=target.at[lon],
-                    send_sem=lon_send.at[phase, s], recv_sem=lon_recv.at[phase, s],
+                    send_sem=lon_send.at[phase, g, s], recv_sem=lon_recv.at[phase, g, s],
                     device_id=(lat, peer), device_id_type=MESH,
                 )
             )
             copies[-1].start()
         return copies
 
-    def spread(phase, buffer):
+    def spread(phase, g, buffer):
         copies = []
         for s, peer in enumerate(lat_peers):
             copies.append(
                 pltpu.make_async_remote_copy(
                     src_ref=buffer.at[lat], dst_ref=buffer.at[lat],
-                    send_sem=lat_send.at[phase, s], recv_sem=lat_recv.at[phase, s],
+                    send_sem=lat_send.at[phase, g, s], recv_sem=lat_recv.at[phase, g, s],
                     device_id=(peer, lon), device_id_type=MESH,
                 )
             )
@@ -254,73 +260,96 @@
 
     def finish(copies):
         for copy in copies:
-            copy.wait()
-
-    def lane_block(part):
-        return pl.ds(pl.multiple_of(part * chunk, LANES), chunk)
+            copy.wait_recv()
+        started.extend(copies)
 
     def both(table, data):
         first = jnp.dot(table[0], data, preferred_element_type=f32)
         return first + jnp.dot(table[1], data, preferred_element_type=f32)
 
-    copies = scatter(0, lambda peer: flat.at[:, lane_block(peer)], columns)
-    columns[lon] = flat[:, lane_block(lon)]
-    finish(copies)
-    spectrum = both(fwd_ref, columns[...].reshape(lon_parts * pad, chunk))
-    spec_out[...] = spectrum.astype(bf16).reshape(spec_out.shape)
-    copies = scatter(1, lambda peer: spec_out.at[peer], spec_in)
-    spec_in[lon] = spec_out[lon]
-    finish(copies)
-    for i in range(rows):
-        for c in range(tiles):
-            part, tile = divmod(i * tiles + c, per)
-            piece = spec_in[part, :, pl.ds(tile * LANES, LANES)].astype(f32)
+    started = []
+    every = range(len(groups))
+    moving = []
+    for g in every:
+        first, last, per = groups[g]
+        used = rows * (last - first) * LANES
+        for i in range(rows):
+            for c in range(first, last):
+                spot_at = (i * (last - first) + c - first) * LANES
+                flat[g][:, pl.ds(spot_at, LANES)] = jnp.where(
+                    spot[:, :LANES] < cols, state[i, :, pl.ds(c * LANES, LANES)], 0.0
+                ).astype(bf16)
+        tail = flat[g].shape[1] - used
+        if tail:
+            flat[g][:, pl.ds(used, tail)] = jnp.zeros((pad, tail), bf16)
+        moving.append(scatter(0, g, lambda peer: flat[g].at[:, chunk(g, peer)], columns[g]))
+        columns[g][lon] = flat[g][:, chunk(g, lon)]
+    for g in every:
+        finish(moving[g])
+        spectrum = both(fwd_ref, columns[g][...].reshape(lon_parts * pad, -1))
+        spec_out[g][...] = spectrum.astype(bf16).reshape(spec_out[g].shape)
+        moving[g] = scatter(1, g, lambda peer: spec_out[g].at[peer], spec_in[g])
+        spec_in[g][lon] = spec_out[g][lon]
+    for g in every:
+        finish(moving[g])
+        for i, c, part, at in cells(g):
+            piece = spec_in[g][part, :, at].astype(f32)
             packed[pl.ds(i * modes, modes), pl.ds(c * LANES, LANES)] = piece[:modes]
-    lat_spec[lat] = packed[pl.ds(0, rows * modes), :].astype(bf16)
-    finish(spread(0, lat_spec))
-    coefficients = both(analysis, lat_spec[...].reshape(total_rows * modes, channels))
-    loads[2].wait()
+        lat_spec[g][lat] = packed[pl.ds(0, rows * modes), width(g)].astype(bf16)
+        moving[g] = spread(0, g, lat_spec[g])
     shape = (modes, keep_ref.shape[1])
     order = 2 * lax.broadcasted_iota(jnp.int32, shape, 1)
     mode = lax.broadcasted_iota(jnp.int32, shape, 0)
     mine = (mode >= order) & (mode < order + 2)
+    for g in every:
+        finish(moving[g])
+        gathered = lat_spec[g][...].reshape(total_rows * modes, -1)
+        packed[pl.ds(0, degrees * modes), width(g)] = both(analysis, gathered)
+    loads[2].wait()
     for l in range(degrees):
+        at = pl.ds(l * modes, modes)
         kept = jnp.where(mine, keep_ref[l : l + 1, :].astype(f32), 0.0)
-        mixed = jnp.dot(
-            coefficients[l * modes : (l + 1) * modes].astype(bf16), fw[l],
-            preferred_element_type=f32,
+        kept = jnp.sum(kept, axis=1, keepdims=True)
+        mixed[at, :] = jnp.broadcast_to(kept, (modes, channels))
+    for g in every:
+        for l in range(degrees):
+            at = pl.ds(l * modes, modes)
+            product = jnp.dot(
+                packed[at, :].astype(bf16), fw[l, :, width(g)], preferred_element_type=f32
+            )
+            mixed[at, width(g)] = product * mixed[at, width(g)]
+        lat_filt[g][lat] = mixed[pl.ds(0, degrees * modes), width(g)].astype(bf16)
+        moving[g] = spread(1, g, lat_filt[g])
+    over = (((0,), (0,)), ((), ()))
+    packed[pl.ds(rows * modes, mode_pad), :] = jnp.zeros((mode_pad, channels), f32)
+    for g in every:
+        finish(moving[g])
+        filtered = lat_filt[g][...].reshape(total_degrees * modes, -1)
+        packed[pl.ds(0, rows * modes), width(g)] = sum(
+            lax.dot_general(rebuild[n], filtered, over, preferred_element_type=f32)
+            for n in range(2)
         )
-        packed[pl.ds(l * modes, modes), :] = mixed * jnp.sum(kept, axis=1, keepdims=True)
-    lat_filt[lat] = packed[pl.ds(0, degrees * modes), :].astype(bf16)
-    finish(spread(1, lat_filt))
-    filtered = lat_filt[...].reshape(total_degrees * modes, channels)
-    over = (((0,), (0,)), ((), ()))
-    packed[pl.ds(0, rows * modes), :] = sum(
-        lax.dot_general(rebuild[n], filtered, over, preferred_element_type=f32)
-        for n in range(2)
-    )
-    packed[pl.ds(rows * modes, mode_pad), :] = jnp.zeros((mode_pad, channels), f32)
-    syn_out[...] = jnp.zeros(syn_out.shape, bf16)
-    for i in range(rows):
-        for c in range(tiles):
-            part, tile = divmod(i * tiles + c, per)
-            syn_out[part, :, pl.ds(tile * LANES, LANES)] = packed[
+        syn_out[g][...] = jnp.zeros(syn_out[g].shape, bf16)
+        for i, c, part, at in cells(g):
+            syn_out[g][part, :, at] = packed[
                 pl.ds(i * modes, mode_pad), pl.ds(c * LANES, LANES)
             ].astype(bf16)
-    copies = scatter(2, lambda peer: syn_out.at[peer], syn_in)
-    syn_in[lon] = syn_out[lon]
-    finish(copies)
-    physical = both(inv_ref, syn_in[...].reshape(lon_parts * mode_pad, chunk))
-    phys_out[...] = physical.astype(bf16).reshape(phys_out.shape)
-    copies = scatter(3, lambda peer: phys_out.at[peer], phys_in)
-    phys_in[lon] = phys_out[lon]
-    finish(copies)
-    for i in range(rows):
-        for c in range(tiles):
-            part, tile = divmod(i * tiles + c, per)
-            at = pl.ds(c * LANES, LANES)
-            value = phys_in[part, :, pl.ds(tile * LANES, LANES)].astype(f32)
-            out_ref[i, :, at] = (state[i, :, at] + gelu(value))[:cols]
+        moving[g] = scatter(2, g, lambda peer: syn_out[g].at[peer], syn_in[g])
+        syn_in[g][lon] = syn_out[g][lon]
+    for g in every:
+        finish(moving[g])
+        physical = both(inv_ref, syn_in[g][...].reshape(lon_parts * mode_pad, -1))
+        phys_out[g][...] = physical.astype(bf16).reshape(phys_out[g].shape)
+        moving[g] = scatter(3, g, lambda peer: phys_out[g].at[peer], phys_in[g])
+        phys_in[g][lon] = phys_out[g][lon]
+    for g in every:
+        finish(moving[g])
+        for i, c, part, at in cells(g):
+            here = pl.ds(c * LANES, LANES)
+            value = phys_in[g][part, :, at].astype(f32)
+            out_ref[i, :, here] = (state[i, :, here] + gelu(value))[:cols]
+    for copy in started:
+        copy.wait_send()
 
 
 def per_device(grid_state, norm_gain, conv_weight, filter_weight, degree_keep):
@@ -330,17 +359,30 @@
     modes = 2 * orders
     col_pad, mode_pad = up(cols, 16), up(modes, 16)
     col_rows = up(rows, 8)
-    chunk = up(-(-rows * channels // lon_parts), LANES)
+    tiles = channels // LANES
+    middle = (2 * tiles + 2) // 3
+    groups = tuple(
+        (first, last, -(-rows * (last - first) // lon_parts))
+        for first, last in ((0, middle), (middle, tiles))
+        if last > first
+    )
     total_rows, total_degrees = rows * lat_parts, degrees * lat_parts
     vmem = pl.BlockSpec(memory_space=pltpu.VMEM)
     hbm = pl.BlockSpec(memory_space=pl.ANY)
     dma = pltpu.SemaphoreType.DMA
     forward, inverse = fourier_tables(lon_parts, cols, col_pad, orders, mode_pad)
     seeds, lines = legendre_seeds(lon_parts, orders, modes, total_degrees, total_rows)
-    block = pltpu.VMEM((lon_parts, mode_pad, chunk), bf16)
-    column_block = pltpu.VMEM((lon_parts, col_pad, chunk), bf16)
+
+    def each(shape_of):
+        return tuple(
+            pltpu.VMEM(shape_of(per * LANES, (last - first) * LANES), bf16)
+            for first, last, per in groups
+        )
+
+    block = each(lambda chunk, width: (lon_parts, mode_pad, chunk))
+    column_block = each(lambda chunk, width: (lon_parts, col_pad, chunk))
     return pl.pallas_call(
-        functools.partial(block_kernel, lat_parts, lon_parts, chunk, modes),
+        functools.partial(block_kernel, lat_parts, lon_parts, groups, modes),
         out_shape=jax.ShapeDtypeStruct((rows, cols, channels), f32),
         in_specs=[vmem] * 7 + [hbm, hbm],
         out_specs=vmem,
@@ -352,12 +394,12 @@
             pltpu.VMEM((2, 2, col_rows, channels), f32),
             pltpu.VMEM((2, 2, col_pad, channels), bf16),
             pltpu.VMEM((2, 4, 8, channels), f32),
-            pltpu.VMEM((col_pad, lon_parts * chunk), bf16),
+            each(lambda chunk, width: (col_pad, lon_parts * chunk)),
             column_block,
             block,
             block,
-            pltpu.VMEM((lat_parts, rows * modes, channels), bf16),
-            pltpu.VMEM((lat_parts, degrees * modes, channels), bf16),
+            each(lambda chunk, width: (lat_parts, rows * modes, width)),
+            each(lambda chunk, width: (lat_parts, degrees * modes, width)),
             block,
             block,
             column_block,
@@ -366,15 +408,16 @@
             pltpu.VMEM((2, degrees * modes, total_rows * modes), bf16),
             pltpu.VMEM((2, total_degrees * modes, rows * modes), bf16),
             pltpu.VMEM((max(rows, degrees) * modes + mode_pad, channels), f32),
+            pltpu.VMEM((degrees * modes, channels), f32),
             pltpu.VMEM((degrees, channels, channels), bf16),
             dma((2,)),
             dma(()),
             dma((2, 8)),
             dma((2, 8)),
-            dma((4, lon_parts - 1)),
-            dma((4, lon_parts - 1)),
-            dma((2, lat_parts - 1)),
-            dma((2, lat_parts - 1)),
+            dma((4, len(groups), lon_parts - 1)),
+            dma((4, len(groups), lon_parts - 1)),
+            dma((2, len(groups), lat_parts - 1)),
+            dma((2, len(groups), lat_parts - 1)),
         ],
         compiler_params=pltpu.CompilerParams(collective_id=0, has_side_effects=True),
         name="block",

time: 57.1 us -> 55.6 us (0.974)
  Pallas kernels: 53.9 us -> 52.3 us
    pallas_call x1, Pallas kernels: 53.9 us -> 52.3 us  [per_device(): pl.pallas_call(functools.partial(block_kernel, lat_parts, lon_parts, grou...]
where the time goes in v3:
time: 55.6 us; the launch traced here: 55.4 us
  Pallas kernels  52.3 us (94%)
  local copies, waits for them, and re-layouts  3.06 us (6%)
    pallas_call x1, Pallas kernels, per_device(): pl.pallas_call(functools.partial(block_kernel, lat_parts, lon_parts, grou...  52.3 us
    unnamed x2, local copies, waits for them, and re-layouts  3.06 us

profile of v3, /device:TPU:0, one launch (start us, length us, event | category | flops | bytes accessed | tf_op | source)
XLA Modules:
  0.0 55.4 jit_solution(3272403563710723753)
XLA Ops:
  0.0 1.4 %copy.10.keep_ref = s32[12,6]{1,0:T(8,128)} copy(s32[12,6]{0,1:T(8,128)} %param.13) | data formatting | bytes 576 | tf_op args[4]
  1.4 52.3 %block.1 = f32[12,15,384]{2,1,0:T(8,128)} custom-call(f32[12,15,384]{2,1,0:T(8,128)} %x_ref.1, f32[2,384]{1,0:T(2,128)} %gain_ref.1, s32[12,6]{1,0:T(8,128)} %copy.10.keep_ref, bf16[2,128,128]{2,1,0:T(8,128)(2,1)} %constant.8.clone.fwd_ref, bf16[2,128,128]{2,1,0:T(8,128)(2,1)} %constant.9.clone.inv_ref, f32[8,16,192]{2,1,0:T(8,128)} %constant.10.clone.seed_ref, ...), custom_call_target="tpu_custom_call" | custom-call | tf_op jit(solution)/shard_map/block/pallas_call | solution.py:384
  53.7 1.7 %copy.12 = f32[12,15,384]{2,1,0:T(8,128)} copy(f32[12,15,384]{2,1,0:T(8,128)} %block.1) | data formatting | bytes 552960

commit v4 on v3

--- a/solution.py
+++ b/solution.py
@@ -74,11 +74,12 @@
 
 def block_kernel(
     lat_parts, lon_parts, groups, modes,
-    x_ref, gain_ref, keep_ref, fwd_ref, inv_ref, seed_ref, line_ref, w_hbm, fw_hbm, out_ref,
+    x_hbm, gain_hbm, keep_hbm, fwd_hbm, inv_hbm, seed_hbm, line_hbm, w_hbm, fw_hbm, out_ref,
+    x_ref, gain_ref, keep_ref, fwd_ref, inv_ref, seed_ref, line_ref,
     state, taps, weights, col_send, col_recv, row_recv, corners, flat,
     columns, spec_out, spec_in, lat_spec, lat_filt, syn_out, syn_in, phys_out, phys_in,
     basis, analysis, rebuild, packed, mixed, fw,
-    w_sem, fw_sem, send_sem, recv_sem, lon_send, lon_recv, lat_send, lat_recv,
+    in_sem, w_sem, fw_sem, send_sem, recv_sem, lon_send, lon_recv, lat_send, lat_recv,
 ):
     rows, cols, channels = x_ref.shape
     pad = state.shape[1]
@@ -88,18 +89,22 @@
     total_rows = rows * lat_parts
     total_degrees = degrees * lat_parts
     lat, lon = lax.axis_index("lat"), lax.axis_index("lon")
-    loads = [
-        pltpu.make_async_copy(w_hbm.at[k], weights.at[k], w_sem.at[k]) for k in range(2)
-    ]
-    loads.append(pltpu.make_async_copy(fw_hbm, fw, fw_sem))
-    for load in loads:
-        load.start()
     north = lax.rem(lat + lat_parts - 1, lat_parts)
     south = lax.rem(lat + 1, lat_parts)
     west = lax.rem(lon + lon_parts - 1, lon_parts)
     east = lax.rem(lon + 1, lon_parts)
     lon_peers = [lax.rem(lon + s, lon_parts) for s in range(1, lon_parts)]
     lat_peers = [lax.rem(lat + s, lat_parts) for s in range(1, lat_parts)]
+    if lat_parts == 4:
+        lat_peers = [
+            3 - lat, lat + 1 - 2 * lax.rem(lat, 2), lax.rem(lat + 2, 4),
+        ]
+    far_first = []
+    for n in range(lon_parts - 1):
+        down, rise = lon_parts - 1 - n, n
+        down = jnp.where(down <= lon, down - 1, down)
+        rise = jnp.where(rise >= lon, rise + 1, rise)
+        far_first.append(jnp.where(2 * lon < lon_parts, down, rise))
     corner_peers = [(north, west), (south, west), (north, east), (south, east)]
     around = [(north, lon), (south, lon), (lat, west), (lat, east)] + corner_peers
     greeted = [(lat, peer) for peer in lon_peers] + [(peer, lon) for peer in lat_peers]
@@ -107,14 +112,30 @@
     barrier = pltpu.get_barrier_semaphore()
     for device in greeted:
         pl.semaphore_signal(barrier, inc=1, device_id=device, device_id_type=MESH)
+    pairs = [
+        (x_hbm, x_ref), (gain_hbm, gain_ref), (seed_hbm.at[lon], seed_ref),
+        (line_hbm, line_ref), (fwd_hbm, fwd_ref), (keep_hbm, keep_ref), (inv_hbm, inv_ref),
+    ]
+    inputs = [
+        pltpu.make_async_copy(source, target, in_sem.at[n])
+        for n, (source, target) in enumerate(pairs)
+    ]
+    loads = [
+        pltpu.make_async_copy(w_hbm.at[k], weights.at[k], w_sem.at[k]) for k in range(2)
+    ]
+    loads.append(pltpu.make_async_copy(fw_hbm, fw, fw_sem))
+    for load in inputs + loads:
+        load.start()
     spot = lax.broadcasted_iota(jnp.int32, (pad, channels), 0)
+    col_send[...] = jnp.zeros(col_send.shape, f32)
+    for load in inputs[:2]:
+        load.wait()
     for r in range(rows):
         state[r, pl.ds(cols, pad - cols), :] = jnp.zeros((pad - cols, channels), f32)
         state[r, pl.ds(0, cols), :] = x_ref[r]
-    col_send[...] = jnp.zeros(col_send.shape, f32)
 
     def legendre():
-        seeds = seed_ref[lon]
+        seeds = seed_ref[...]
         growth = seeds[:, :total_degrees]
         damping = seeds[:, total_degrees : 2 * total_degrees]
         start = seeds[:, 2 * total_degrees : 3 * total_degrees]
@@ -182,6 +203,8 @@
         for n in (4, 5, 6, 7, 0, 1, 2, 3):
             copies[n].start()
         if k == 0:
+            for load in inputs[2:]:
+                load.wait()
             legendre()
             own_rows = pl.ds(pl.multiple_of(lat * degrees * modes, 8), degrees * modes)
             expand(basis[own_rows, :] * line_ref[1:2, :], 0, analysis)
@@ -233,17 +256,25 @@
         return pl.ds(pl.multiple_of(part * size, LANES), size)
 
     def scatter(phase, g, source_of, target):
-        copies = []
-        for s, peer in enumerate(lon_peers):
-            copies.append(
-                pltpu.make_async_remote_copy(
-                    src_ref=source_of(peer), dst_ref=target.at[lon],
-                    send_sem=lon_send.at[phase, g, s], recv_sem=lon_recv.at[phase, g, s],
-                    device_id=(lat, peer), device_id_type=MESH,
-                )
-            )
-            copies[-1].start()
-        return copies
+        sends = [
+            pltpu.make_async_remote_copy(
+                src_ref=source_of(peer), dst_ref=target.at[lon],
+                send_sem=lon_send.at[phase, g, s], recv_sem=lon_recv.at[phase, g, lon],
+                device_id=(lat, peer), device_id_type=MESH,
+            )
+            for s, peer in enumerate(far_first)
+        ]
+        for copy in sends:
+            copy.start()
+        started.extend(sends)
+        return [
+            pltpu.make_async_remote_copy(
+                src_ref=target.at[peer], dst_ref=target.at[peer],
+                send_sem=lon_send.at[phase, g, s], recv_sem=lon_recv.at[phase, g, peer],
+                device_id=(lat, peer), device_id_type=MESH,
+            )
+            for s, peer in enumerate(lon_peers)
+        ]
 
     def spread(phase, g, buffer):
         copies = []
@@ -256,12 +287,12 @@
                 )
             )
             copies[-1].start()
+        started.extend(copies)
         return copies
 
     def finish(copies):
         for copy in copies:
             copy.wait_recv()
-        started.extend(copies)
 
     def both(table, data):
         first = jnp.dot(table[0], data, preferred_element_type=f32)
@@ -384,9 +415,16 @@
     return pl.pallas_call(
         functools.partial(block_kernel, lat_parts, lon_parts, groups, modes),
         out_shape=jax.ShapeDtypeStruct((rows, cols, channels), f32),
-        in_specs=[vmem] * 7 + [hbm, hbm],
+        in_specs=[hbm] * 9,
         out_specs=vmem,
         scratch_shapes=[
+            pltpu.VMEM((rows, cols, channels), f32),
+            pltpu.VMEM(norm_gain.shape, f32),
+            pltpu.VMEM(degree_keep.shape, degree_keep.dtype),
+            pltpu.VMEM(forward.shape, bf16),
+            pltpu.VMEM(inverse.shape, bf16),
+            pltpu.VMEM(seeds.shape[1:], f32),
+            pltpu.VMEM(lines.shape, f32),
             pltpu.VMEM((rows, col_pad, channels), f32),
             pltpu.VMEM((2, 3, (rows + 2) * col_pad, channels), bf16),
             pltpu.VMEM((2, 3, 3, channels, channels), bf16),
@@ -410,12 +448,13 @@
             pltpu.VMEM((max(rows, degrees) * modes + mode_pad, channels), f32),
             pltpu.VMEM((degrees * modes, channels), f32),
             pltpu.VMEM((degrees, channels, channels), bf16),
+            dma((7,)),
             dma((2,)),
             dma(()),
             dma((2, 8)),
             dma((2, 8)),
             dma((4, len(groups), lon_parts - 1)),
-            dma((4, len(groups), lon_parts - 1)),
+            dma((4, len(groups), lon_parts)),
             dma((2, len(groups), lat_parts - 1)),
             dma((2, len(groups), lat_parts - 1)),
         ],

time: 55.6 us -> 54.7 us (0.984)
  Pallas kernels: 52.3 us -> 51.5 us
    pallas_call x1, Pallas kernels: 52.3 us -> 51.5 us  [per_device(): pl.pallas_call(functools.partial(block_kernel, lat_parts, lon_parts, grou...]
where the time goes in v4:
time: 54.7 us; the launch traced here: 54.5 us
  Pallas kernels  51.5 us (94%)
  local copies, waits for them, and re-layouts  3.06 us (6%)
    pallas_call x1, Pallas kernels, per_device(): pl.pallas_call(functools.partial(block_kernel, lat_parts, lon_parts, grou...  51.5 us
    unnamed x2, local copies, waits for them, and re-layouts  3.06 us

profile of v4, /device:TPU:0, one launch (start us, length us, event | category | flops | bytes accessed | tf_op | source)
XLA Modules:
  0.0 54.5 jit_solution(4836030273462331941)
XLA Ops:
  0.0 1.4 %copy.10.keep_hbm = s32[12,6]{1,0:T(8,128)} copy(s32[12,6]{0,1:T(8,128)} %param.13) | data formatting | bytes 576 | tf_op args[4]
  1.4 51.5 %block.1 = f32[12,15,384]{2,1,0:T(8,128)} custom-call(f32[12,15,384]{2,1,0:T(8,128)} %x_hbm.1, f32[2,384]{1,0:T(2,128)} %gain_hbm.1, s32[12,6]{1,0:T(8,128)} %copy.10.keep_hbm, bf16[2,128,128]{2,1,0:T(8,128)(2,1)} %constant.8.clone.fwd_hbm, bf16[2,128,128]{2,1,0:T(8,128)(2,1)} %constant.9.clone.inv_hbm, f32[8,16,192]{2,1,0:T(8,128)} %constant.10.clone.seed_hbm, ...), custom_call_target="tpu_custom_call" | custom-call | tf_op jit(solution)/shard_map/block/pallas_call | solution.py:415
  52.8 1.7 %copy.12 = f32[12,15,384]{2,1,0:T(8,128)} copy(f32[12,15,384]{2,1,0:T(8,128)} %block.1) | data formatting | bytes 552960

commit v5 on v4

--- a/solution.py
+++ b/solution.py
@@ -210,14 +210,18 @@
             expand(basis[own_rows, :] * line_ref[1:2, :], 0, analysis)
         else:
             expand(basis[...], lat * rows, rebuild)
+        for r in range(rows):
+            at = pl.ds((r + 1) * pad, pad)
+            wide = taps[k, 1, at, :].astype(f32)
+            taps[k, 0, at, :] = pltpu.roll(wide, 1, 0).astype(bf16)
+            taps[k, 2, at, :] = pltpu.roll(wide, pad - 1, 0).astype(bf16)
         loads[k].wait()
         for copy in copies:
             copy.wait()
         for r in range(rows):
-            place(
-                k, r + 1, taps[k, 1, pl.ds((r + 1) * pad, pad), :].astype(f32),
-                col_recv[k, 0, pl.ds(r, 1), :], col_recv[k, 1, pl.ds(r, 1), :],
-            )
+            base = (r + 1) * pad
+            taps[k, 0, pl.ds(base, 1), :] = col_recv[k, 0, pl.ds(r, 1), :].astype(bf16)
+            taps[k, 2, pl.ds(base + cols - 1, 1), :] = col_recv[k, 1, pl.ds(r, 1), :].astype(bf16)
         low = rows - 1 - (col_rows - 8)
         for side, line, inside, west_at, east_at, row in (
             (0, 0, lat > 0, 3, 1, low),
@@ -391,7 +395,7 @@
     col_pad, mode_pad = up(cols, 16), up(modes, 16)
     col_rows = up(rows, 8)
     tiles = channels // LANES
-    middle = (2 * tiles + 2) // 3
+    middle = tiles // 3
     groups = tuple(
         (first, last, -(-rows * (last - first) // lon_parts))
         for first, last in ((0, middle), (middle, tiles))

time: 54.7 us -> 53.8 us (0.984)
  Pallas kernels: 51.5 us -> 50.6 us
    pallas_call x1, Pallas kernels: 51.5 us -> 50.6 us  [per_device(): pl.pallas_call(functools.partial(block_kernel, lat_parts, lon_parts, grou...]
where the time goes in v5:
time: 53.8 us; the launch traced here: 53.7 us
  Pallas kernels  50.6 us (94%)
  local copies, waits for them, and re-layouts  3.06 us (6%)
    pallas_call x1, Pallas kernels, per_device(): pl.pallas_call(functools.partial(block_kernel, lat_parts, lon_parts, grou...  50.6 us
    unnamed x2, local copies, waits for them, and re-layouts  3.06 us

profile of v5, /device:TPU:0, one launch (start us, length us, event | category | flops | bytes accessed | tf_op | source)
XLA Modules:
  0.0 53.7 jit_solution(12343956321302724384)
XLA Ops:
  0.0 1.4 %copy.10.keep_hbm = s32[12,6]{1,0:T(8,128)} copy(s32[12,6]{0,1:T(8,128)} %param.13) | data formatting | bytes 576 | tf_op args[4]
  1.4 50.6 %block.1 = f32[12,15,384]{2,1,0:T(8,128)} custom-call(f32[12,15,384]{2,1,0:T(8,128)} %x_hbm.1, f32[2,384]{1,0:T(2,128)} %gain_hbm.1, s32[12,6]{1,0:T(8,128)} %copy.10.keep_hbm, bf16[2,128,128]{2,1,0:T(8,128)(2,1)} %constant.8.clone.fwd_hbm, bf16[2,128,128]{2,1,0:T(8,128)(2,1)} %constant.9.clone.inv_hbm, f32[8,16,192]{2,1,0:T(8,128)} %constant.10.clone.seed_hbm, ...), custom_call_target="tpu_custom_call" | custom-call | tf_op jit(solution)/shard_map/block/pallas_call | solution.py:419
  52.0 1.7 %copy.12 = f32[12,15,384]{2,1,0:T(8,128)} copy(f32[12,15,384]{2,1,0:T(8,128)} %block.1) | data formatting | bytes 552960
